TPU v7x, 512 devices: a whole 4x8x8 slice. The times are simulated.
512 devices in a mesh: dom: 128 (over y, z, core), rep: 4 (over x).
Axes of the slice: x: 4, y: 8, z: 8, core: 2. Of those that a mesh axis runs over, the one named last changes fastest.
Arguments:
- feats: bfloat16 [131072, 256], P('dom'), may hold values from -6 to 6
- history: bfloat16 [131072, 256], P('dom'), may hold values from -6 to 6
- adj_inner: bfloat16 [131072, 1024], P('dom'), may hold values from -0.15625 to 0.15625
- adj_halo: bfloat16 [131072, 256], P('dom'), may hold values from -0.15625 to 0.15625
- halo_rows: int32 [16384, 2], P('dom'), may hold values from 0 to 1023
- w_self: bfloat16 [256, 256], replicated, may hold values from -0.375 to 0.375
- w_nbr: bfloat16 [256, 256], replicated, may hold values from -0.375 to 0.375
- b_enc: float32 [256], replicated, may hold values from -3 to 3
- edge_owner: int32 [131072, 2], P(('dom', 'rep')), may hold values from 0 to 127, all different within a row; in each aligned block of 256 rows (0 to 255, 256 to 511, ...) at most 8 rows name the same one
- edge_rows: int32 [131072, 2], P(('dom', 'rep')), may hold values from 0 to 1023
- labels: int32 [131072], P(('dom', 'rep')), may hold values 0 or 1
- w_dec1: bfloat16 [256, 256], replicated, may hold values from -0.375 to 0.375
- b_dec1: float32 [256], replicated, may hold values from -3 to 3
- w_dec2: bfloat16 [256], replicated, may hold values from -0.375 to 0.375
Outputs:
- embed: bfloat16 [131072, 256], P('dom')
- grad_embed: float32 [131072, 256], P(('dom', 'rep'))
- grad_dec1: float32 [256, 256], replicated
- grad_bias1: float32 [256], replicated
- grad_dec2: float32 [256], replicated
Inputs may be any that keep to these rules, and one draw needn't show every extreme that they name: `edge_owner`: among the rows of one device, no owner is named by more than 8 endpoints, a bound that some block reaches; the two endpoints of an edge have different owners.
All inputs are finite; a program needn't handle non-finite values. No bound on the sum of `labels` on one device may be relied on, other than what follows from the above.
Results may differ from a plain program's by a relative error of at most 0.0069.
Values may be sent and summed in bfloat16 or wider, within the bound.
A program may use at most 64 MiB of HBM per device.

v0:
```python
import jax
import jax.numpy as jnp
from jax import lax
from jax.sharding import PartitionSpec as P


def encode_block(rows_x, a_inner, a_halo, all_x, halo, w_self, w_nbr, b_enc):
    agg = (
        jnp.dot(a_inner, all_x, preferred_element_type=jnp.float32)
        + jnp.dot(a_halo, halo, preferred_element_type=jnp.float32)
    ).astype(jnp.bfloat16)
    pre = (
        jnp.dot(rows_x, w_self, preferred_element_type=jnp.float32)
        + jnp.dot(agg, w_nbr, preferred_element_type=jnp.float32)
        + b_enc
    )
    return jnp.maximum(pre, 0.0).astype(jnp.bfloat16)


def decode(head, tail, target, w_dec1, b_dec1, w_dec2):
    zprod = (head.astype(jnp.float32) * tail.astype(jnp.float32)).astype(jnp.bfloat16)
    pre = jnp.dot(zprod, w_dec1, preferred_element_type=jnp.float32) + b_dec1
    sig = jax.nn.sigmoid(pre)
    hidden = (pre * sig).astype(jnp.bfloat16)
    logit = jnp.dot(hidden, w_dec2, preferred_element_type=jnp.float32)
    dlogit = jax.nn.sigmoid(logit) - target
    d_pre = (
        dlogit[:, None] * w_dec2.astype(jnp.float32) * (sig * (1.0 + pre * (1.0 - sig)))
    ).astype(jnp.bfloat16)
    grad_w1 = jnp.dot(zprod.T, d_pre, preferred_element_type=jnp.float32)
    grad_b1 = jnp.sum(d_pre.astype(jnp.float32), axis=0)
    grad_w2 = jnp.sum(hidden.astype(jnp.float32) * dlogit[:, None], axis=0)
    dzval = jnp.dot(d_pre, w_dec1.T, preferred_element_type=jnp.float32)
    return (
        dzval * tail.astype(jnp.float32),
        dzval * head.astype(jnp.float32),
        grad_w1,
        grad_b1,
        grad_w2,
    )


def per_device(
    feats,
    history,
    adj_inner,
    adj_halo,
    halo_rows,
    w_self,
    w_nbr,
    b_enc,
    edge_owner,
    edge_rows,
    labels,
    w_dec1,
    b_dec1,
    w_dec2,
):
    n_dom = lax.axis_size("dom")
    nodes = feats.shape[0]
    width = feats.shape[1]
    halo = lax.all_to_all(
        history[lax.all_to_all(halo_rows, "dom", split_axis=0, concat_axis=0, tiled=True)],
        "dom",
        split_axis=0,
        concat_axis=0,
        tiled=True,
    ).reshape(-1, width)
    embed = encode_block(feats, adj_inner, adj_halo, feats, halo, w_self, w_nbr, b_enc)
    queries = edge_owner.shape[0]
    cap_edge = max(2, 4 * queries // n_dom)
    owners = edge_owner.reshape(-1)
    local = edge_rows.reshape(-1)
    match = (owners[:, None] == jnp.arange(n_dom, dtype=jnp.int32)[None, :]).astype(jnp.int32)
    slots = jnp.sum(jnp.cumsum(match, axis=0) * match, axis=1) - 1
    place = owners * cap_edge + slots
    send_ids = (
        jnp.zeros((n_dom * cap_edge,), jnp.int32).at[place].set(local).reshape(n_dom, cap_edge)
    )
    wanted = lax.all_to_all(send_ids, "dom", split_axis=0, concat_axis=0, tiled=True)
    fetched = lax.all_to_all(embed[wanted], "dom", split_axis=0, concat_axis=0, tiled=True)
    ends = fetched.reshape(-1, width)[place].reshape(queries, 2, width)
    target = labels.astype(jnp.float32)
    g_head, g_tail, gw1, gb1, gw2 = decode(ends[:, 0], ends[:, 1], target, w_dec1, b_dec1, w_dec2)
    grads = jnp.stack([g_head, g_tail], axis=1).reshape(-1, width)
    send_grads = jnp.zeros((n_dom * cap_edge, width), jnp.float32).at[place].set(grads)
    back = lax.all_to_all(
        send_grads.reshape(n_dom, cap_edge, width), "dom", split_axis=0, concat_axis=0, tiled=True
    )
    local_grad = (
        jnp.zeros((nodes, width), jnp.float32).at[wanted.reshape(-1)].add(back.reshape(-1, width))
    )
    grad_embed = lax.psum_scatter(local_grad, "rep", scatter_dimension=0, tiled=True)
    grad_dec1, grad_bias1, grad_dec2 = lax.psum((gw1, gb1, gw2), ("dom", "rep"))
    return (embed, grad_embed, grad_dec1, grad_bias1, grad_dec2)


def solution(mesh):
    placed = (
        P("dom", None),
        P("dom", None),
        P("dom", None),
        P("dom", None),
        P("dom", None),
        P(),
        P(),
        P(),
        P(("dom", "rep"), None),
        P(("dom", "rep"), None),
        P(("dom", "rep")),
        P(),
        P(),
        P(),
    )
    return jax.shard_map(
        per_device,
        mesh=mesh,
        in_specs=placed,
        out_specs=(P("dom", None), P(("dom", "rep"), None), P(), P(), P()),
        check_vma=False,
    )
```

profile of v0, /device:TPU:1, one launch (start us, length us, event | category | flops | bytes accessed | tf_op | source)
XLA Modules:
  0.0 414.0 jit_solution(18180660561444571792)
XLA Ops:
  8.0 1.6 copy.30
  9.6 18.4 %all-to-all-start = ((s32[128,1,2]{2,1,0:T(1,128)}), s32[128,1,2]{2,1,0:T(1,128)S(1)}, u32[]{:S(2)}, u32[]{:S(2)}) async-start(s32[128,1,2]{2,1,0:T(1,128)} %bitcast), calls=%async_computation | async-start | bytes 131072 | tf_op jit(solution)/shard_map/all_to_all | solution.py:63
  30.8 1.7 fusion.21
  32.6 1.3 fusion.20
  34.2 2.4 scatter_custom_fusion
  37.3 2.1 all-to-all-done
  39.5 11.6 %all-to-all-start.2 = ((s32[128,1,8]{2,1,0:T(1,128)}), s32[128,1,8]{2,1,0:T(1,128)S(1)}, u32[]{:S(2)}, u32[]{:S(2)}) async-start(s32[128,1,8]{2,1,0:T(1,128)} %bitcast.8), calls=%async_computation.2 | async-start | bytes 131072 | tf_op jit(solution)/shard_map/all_to_all | solution.py:80
  51.3 1.2 gather_fusion
  53.1 9.4 %all-to-all-done.2 = s32[128,1,8]{2,1,0:T(1,128)S(1)} async-done(((s32[128,1,8]{2,1,0:T(1,128)}), s32[128,1,8]{2,1,0:T(1,128)S(1)}, u32[]{:S(2)}, u32[]{:S(2)}) %all-to-all-start.2) | async-done | bytes 4128 | tf_op jit(solution)/shard_map/all_to_all | solution.py:80
  62.5 5.7 %all-to-all-start.1 = ((bf16[128,2,256]{2,1,0:T(2,128)(2,1)}), bf16[128,2,256]{2,1,0:T(2,128)(2,1)S(1)}, u32[]{:S(2)}, u32[]{:S(2)}) async-start(bf16[128,2,256]{2,1,0:T(2,128)(2,1)} %reshape.196), calls=%async_computation.1 | async-start | bytes 262144 | tf_op jit(solution)/shard_map/all_to_all | solution.py:62
  68.4 12.2 %all-to-all-done.1 = bf16[128,2,256]{2,1,0:T(2,128)(2,1)S(1)} async-done(((bf16[128,2,256]{2,1,0:T(2,128)(2,1)}), bf16[128,2,256]{2,1,0:T(2,128)(2,1)S(1)}, u32[]{:S(2)}, u32[]{:S(2)}) %all-to-all-start.1) | async-done | bytes 131104 | tf_op jit(solution)/shard_map/all_to_all | solution.py:62
  80.7 2.2 fusion.3
  82.9 5.0 %gather_fusion.1 = bf16[1024,256]{1,0:T(8,128)(2,1)} fusion(bf16[1024,256]{1,0:T(8,128)(2,1)S(1)} %fusion.3, s32[1024]{0:T(1024)S(1)} %broadcast_clamp_fusion), kind=kCustom, calls=%fused_computation.1 | custom fusion | bytes 1052672 | tf_op jit(solution)/shard_map/gather | solution.py:81
  87.8 6.4 %all-to-all-start.3 = ((bf16[128,8,256]{2,1,0:T(8,128)(2,1)}), bf16[128,8,256]{2,1,0:T(8,128)(2,1)S(1)}, u32[]{:S(2)}, u32[]{:S(2)}) async-start(bf16[128,8,256]{2,1,0:T(8,128)(2,1)} %bitcast.11), calls=%async_computation.3 | async-start | bytes 1048576 | tf_op jit(solution)/shard_map/all_to_all | solution.py:81
  94.3 19.5 %all-to-all-done.3 = bf16[128,8,256]{2,1,0:T(8,128)(2,1)S(1)} async-done(((bf16[128,8,256]{2,1,0:T(8,128)(2,1)}), bf16[128,8,256]{2,1,0:T(8,128)(2,1)S(1)}, u32[]{:S(2)}, u32[]{:S(2)}) %all-to-all-start.3) | async-done | bytes 524320 | tf_op jit(solution)/shard_map/all_to_all | solution.py:81
  113.8 1.9 gather_fusion.2
  118.0 3.2 scatter_custom_fusion.1
  121.2 7.1 %all-to-all-start.4 = ((f32[128,8,256]{2,1,0:T(8,128)}), f32[128,8,256]{2,1,0:T(8,128)S(1)}, u32[]{:S(2)}, u32[]{:S(2)}) async-start(f32[128,8,256]{2,1,0:T(8,128)} %bitcast.73), calls=%async_computation.4 | async-start | bytes 2097152 | tf_op jit(solution)/shard_map/all_to_all | solution.py:87
  129.8 0.9 fusion.23
  130.9 27.9 %all-to-all-done.4 = f32[128,8,256]{2,1,0:T(8,128)S(1)} async-done(((f32[128,8,256]{2,1,0:T(8,128)}), f32[128,8,256]{2,1,0:T(8,128)S(1)}, u32[]{:S(2)}, u32[]{:S(2)}) %all-to-all-start.4) | async-done | bytes 1048608 | tf_op jit(solution)/shard_map/all_to_all | solution.py:87
  158.8 7.1 %scatter_custom_fusion.2 = f32[1024,256]{1,0:T(8,128)} fusion(s32[1024]{0:T(1024)S(1)} %bitcast.84, f32[128,8,256]{2,1,0:T(8,128)S(1)} %all-to-all-done.4, f32[]{:T(128)} %constant.8.clone.1), kind=kCustom, calls=%fused_computation.14 | custom fusion | flops 262144 | bytes 2097156 | tf_op jit(solution)/shard_map/scatter-add | solution.py:91
  165.9 97.7 %all-reduce = (f32[256]{0:T(256)}, f32[256]{0:T(256)}) all-reduce(f32[256]{0:T(256)S(1)} %get-tuple-element.7, f32[256]{0:T(256)S(1)} %get-tuple-element.13), channel_id=1, replica_groups=mesh['dom'=128,'rep'=4] {'dom','rep'}, use_global_device_ids=true, to_apply=%region_9.10 | all-reduce | flops 512 | bytes 4096 | tf_op jit(solution)/shard_map/psum | solution.py:94
  263.6 141.3 %all-reduce.3.cloned.1.call-done = f32[256,256]{1,0:T(8,128)} async-done(((f32[256,256]{1,0:T(8,128)}), f32[256,256]{1,0:T(8,128)}) %all-reduce.3.cloned.1.call-update) | async-done | bytes 262160 | tf_op jit(solution)/shard_map/psum | solution.py:94
  404.9 1.7 copy.56
  (77 shorter events, 8.5 us)
Async XLA Ops:
  8.0 22.8 %copy-start = (bf16[1024,1024]{1,0:T(8,128)(2,1)S(1)}, bf16[1024,1024]{1,0:T(8,128)(2,1)}, u32[]{:S(2)}) copy-start(bf16[1024,1024]{1,0:T(8,128)(2,1)} %param.16) | copy-start | bytes 6291460
  8.0 22.8 %copy-start.4 = (bf16[1024,256]{1,0:T(8,128)(2,1)S(1)}, bf16[1024,256]{1,0:T(8,128)(2,1)}, u32[]{:S(2)}) copy-start(bf16[1024,256]{1,0:T(8,128)(2,1)} %param.14) | copy-start | bytes 1572868
  9.6 29.9 %all-to-all-start = ((s32[128,1,2]{2,1,0:T(1,128)}), s32[128,1,2]{2,1,0:T(1,128)S(1)}, u32[]{:S(2)}, u32[]{:S(2)}) async-start(s32[128,1,2]{2,1,0:T(1,128)} %bitcast), calls=%async_computation | async-start | bytes 131072 | tf_op jit(solution)/shard_map/all_to_all | solution.py:63
  30.8 1.8 copy-start.5
  30.8 1.8 copy-start.6
  30.8 3.1 copy-start.8
  32.6 18.7 %copy-start.2 = (bf16[1024,256]{1,0:T(8,128)(2,1)S(1)}, bf16[1024,256]{1,0:T(8,128)(2,1)}, u32[]{:S(2)}) copy-start(bf16[1024,256]{1,0:T(8,128)(2,1)} %param.15) | copy-start | bytes 1572868
  32.6 48.1 %copy-start.3 = (bf16[1024,256]{1,0:T(8,128)(2,1)S(1)}, bf16[1024,256]{1,0:T(8,128)(2,1)}, u32[]{:S(2)}) copy-start(bf16[1024,256]{1,0:T(8,128)(2,1)} %param.17) | copy-start | bytes 1572868
  32.6 48.1 %copy-start.9 = (f32[256]{0:T(256)S(1)}, f32[256]{0:T(256)}, u32[]{:S(2)}) copy-start(f32[256]{0:T(256)} %param.21) | copy-start | bytes 3076
  39.5 23.1 %all-to-all-start.2 = ((s32[128,1,8]{2,1,0:T(1,128)}), s32[128,1,8]{2,1,0:T(1,128)S(1)}, u32[]{:S(2)}, u32[]{:S(2)}) async-start(s32[128,1,8]{2,1,0:T(1,128)} %bitcast.8), calls=%async_computation.2 | async-start | bytes 131072 | tf_op jit(solution)/shard_map/all_to_all | solution.py:80
  62.5 18.0 %all-to-all-start.1 = ((bf16[128,2,256]{2,1,0:T(2,128)(2,1)}), bf16[128,2,256]{2,1,0:T(2,128)(2,1)S(1)}, u32[]{:S(2)}, u32[]{:S(2)}) async-start(bf16[128,2,256]{2,1,0:T(2,128)(2,1)} %reshape.196), calls=%async_computation.1 | async-start | bytes 262144 | tf_op jit(solution)/shard_map/all_to_all | solution.py:62
  82.8 5.0 %copy-start.1 = (bf16[1024,256]{1,0:T(8,128)(2,1)}, bf16[1024,256]{1,0:T(8,128)(2,1)S(1)}, u32[]{:S(2)}) copy-start(bf16[1024,256]{1,0:T(8,128)(2,1)S(1)} %fusion.3) | copy-start | bytes 1572868
  82.8 11.4 %copy-start.12 = (bf16[256]{0:T(256)(128)(2,1)S(1)}, bf16[256]{0:T(256)(128)(2,1)}, u32[]{:S(2)}) copy-start(bf16[256]{0:T(256)(128)(2,1)} %param.27) | copy-start | bytes 1540
  87.8 26.0 %all-to-all-start.3 = ((bf16[128,8,256]{2,1,0:T(8,128)(2,1)}), bf16[128,8,256]{2,1,0:T(8,128)(2,1)S(1)}, u32[]{:S(2)}, u32[]{:S(2)}) async-start(bf16[128,8,256]{2,1,0:T(8,128)(2,1)} %bitcast.11), calls=%async_computation.3 | async-start | bytes 1048576 | tf_op jit(solution)/shard_map/all_to_all | solution.py:81
  113.8 2.5 copy-start.7
  113.8 2.5 copy-start.11
  115.7 1.0 copy-start.10
  121.2 37.5 %all-to-all-start.4 = ((f32[128,8,256]{2,1,0:T(8,128)}), f32[128,8,256]{2,1,0:T(8,128)S(1)}, u32[]{:S(2)}, u32[]{:S(2)}) async-start(f32[128,8,256]{2,1,0:T(8,128)} %bitcast.73), calls=%async_computation.4 | async-start | bytes 2097152 | tf_op jit(solution)/shard_map/all_to_all | solution.py:87
  128.4 276.6 %all-reduce.3.cloned.1.call-start = ((), (), s32[]{:S(2)}) async-start(), calls=%async_computation.7 | async-start | bytes 524288 | tf_op jit(solution)/shard_map/psum | solution.py:94
  130.8 274.1 %reduce-scatter.2.cloned.1.call-start = ((), (), s32[]{:S(2)}) async-start(), calls=%async_computation.6 | async-start | bytes 1310720 | tf_op jit(solution)/shard_map/reduce_scatter | solution.py:93
Sparse Core Ops, SparseCore 0:
  135.5 269.3 all-reduce.2
Sparse Core Ops, SparseCore 1:
  166.0 21.3 reduce-scatter.1
where the time goes:
time: 415 us; the launch traced here: 414 us
  waiting for transfers between devices  212 us (51%)
  blocking collectives  97.7 us (24%)
  starting transfers between devices  49.3 us (12%)
  local copies, waits for them, and re-layouts  22.4 us (5%)
  between operations  15.9 us (4%)
  other arithmetic  9.45 us (2%)
  matrix products  6.73 us (2%)
    psum x1, waiting for transfers between devices, per_device(): grad_dec1, grad_bias1, grad_dec2 = lax.psum((gw1, gb1, gw2), ('dom', 'rep'))  141 us
    psum x1, blocking collectives, per_device(): grad_dec1, grad_bias1, grad_dec2 = lax.psum((gw1, gb1, gw2), ('dom', 'rep'))  97.7 us
    all_to_all x1, waiting for transfers between devices, per_device(): lax.all_to_all(send_grads.reshape(n_dom, cap_edge, width), 'dom', split_a...  27.9 us
    all_to_all x1, waiting for transfers between devices, per_device(): lax.all_to_all(embed[wanted], 'dom', split_axis=0, concat_axis=0, tiled=T...  19.5 us
    all_to_all x1, starting transfers between devices, per_device(): lax.all_to_all(halo_rows, 'dom', split_axis=0, concat_axis=0, tiled=True)  18.4 us
    all_to_all x1, waiting for transfers between devices, per_device(): lax.all_to_all(history[lax.all_to_all(halo_rows, 'dom', split_axis=0, con...  12.2 us
    all_to_all x1, starting transfers between devices, per_device(): lax.all_to_all(send_ids, 'dom', split_axis=0, concat_axis=0, tiled=True)  11.6 us
    all_to_all x1, waiting for transfers between devices, per_device(): lax.all_to_all(send_ids, 'dom', split_axis=0, concat_axis=0, tiled=True)  9.41 us
  transfers between devices with their start and end apart: 7, of which 6 were waited for; matrix products, arithmetic and copies ran while one was open for 5% of the time, Pallas kernels for 0%

commit v1 on v0

v1 whole, which is shorter than its diff:
```python
import functools

import jax
import jax.numpy as jnp
from jax import lax
from jax.experimental import pallas as pl
from jax.experimental.pallas import tpu as pltpu
from jax.sharding import PartitionSpec as P

BF = jnp.bfloat16
F32 = jnp.float32
I32 = jnp.int32
MESH = pl.DeviceIdType.MESH
SLOTS = 8
LANES = 128


def log2(value):
    return value.bit_length() - 1


def iota(shape, dim):
    return lax.broadcasted_iota(I32, shape, dim)


def nn(a, b):
    return lax.dot_general(a, b, (((1,), (0,)), ((), ())), preferred_element_type=F32)


def nt(a, b):
    return lax.dot_general(a, b, (((1,), (1,)), ((), ())), preferred_element_type=F32)


def tn(a, b):
    return lax.dot_general(a, b, (((0,), (0,)), ((), ())), preferred_element_type=F32)


def hot(cond):
    return jnp.where(cond, 1.0, 0.0).astype(BF)


def column_of(row):
    n = row.shape[1]
    return jnp.sum(jnp.where(iota((n, n), 0) == iota((n, n), 1), row, 0.0), axis=1, keepdims=True)


def row_of(column):
    n = column.shape[0]
    return jnp.sum(jnp.where(iota((n, n), 0) == iota((n, n), 1), column, 0.0), axis=0, keepdims=True)


def copies(ref, sem):
    return pltpu.make_async_copy(ref, ref, sem)


def kernel(
    n_y, n_zc, n_x,
    eo, er, hr, lab, b_enc, b_dec1, w_dec2,
    feats_h, hist_h, adji_h, adjh_h, wself_h, wnbr_h, wdec1_h,
    emb_o, ge_o, gd_o, gv_o,
    feats, hist, adji, adjh, wself, wnbr, wdec1,
    ids_s, ids_r1, ids_t, ids_r2,
    hal_s, hal_r1, hal_t, hal_r2, adjp,
    inner, selfp, place,
    hot_e, hot_et, hot_g, hot_gt,
    fet_s, fet_a, fet_b, fet_r,
    gra_s, gra_a, gra_b, gra_r, gpair,
    zbuf, dbuf,
    xs1, xr1, xs2, xr2, xk,
    dc_s, dc_r, dz_s, dz_r, dy_r, dx_r, dg_r,
    load_sem, out_sem,
    ssem, rsem,
):
    n_dom = n_y * n_zc
    nodes, width = feats.shape
    half = width // 2
    queries = eo.shape[1]
    ends = 2 * queries
    slots = n_dom * SLOTS
    halos = 2 * n_dom
    n_z = n_zc // 2
    ly, lzc = log2(n_y), log2(n_zc)
    me = lax.axis_index("dom")
    rep = lax.axis_index("rep")
    y = lax.div(me, n_zc)
    zc = lax.rem(me, n_zc)
    z = lax.div(zc, 2)
    core = lax.rem(zc, 2)

    loads = [
        pltpu.make_async_copy(src, dst, load_sem.at[i])
        for i, (src, dst) in enumerate(
            ((feats_h, feats), (adji_h, adji), (wself_h, wself), (adjh_h, adjh), (hist_h, hist), (wnbr_h, wnbr), (wdec1_h, wdec1))
        )
    ]
    for load in loads:
        load.start()

    barrier = pltpu.get_barrier_semaphore()

    def zc_peer(k):
        return lax.rem(zc + k, n_zc)

    def y_peer(k):
        return lax.rem(y + k, n_y)

    def greet_zc(k, carry):
        pl.semaphore_signal(barrier, inc=1, device_id={"dom": y * n_zc + zc_peer(k)}, device_id_type=MESH)
        return carry

    def greet_y(k, carry):
        pl.semaphore_signal(barrier, inc=1, device_id={"dom": y_peer(k) * n_zc + zc}, device_id_type=MESH)
        return carry

    lax.fori_loop(1, n_zc, greet_zc, 0)
    lax.fori_loop(1, n_y, greet_y, 0)
    for k in range(1, n_x):
        pl.semaphore_signal(barrier, inc=1, device_id={"rep": lax.rem(rep + k, n_x)}, device_id_type=MESH)

    def along_zc(index, source, target):
        def body(k, carry):
            peer = zc_peer(k)
            pltpu.make_async_remote_copy(
                src_ref=source(peer), dst_ref=target(zc), send_sem=ssem.at[index], recv_sem=rsem.at[index],
                device_id={"dom": y * n_zc + peer}, device_id_type=MESH,
            ).start()
            return carry

        lax.fori_loop(1, n_zc, body, 0)
        pltpu.make_async_copy(source(zc), target(zc), rsem.at[index]).start()

    def along_y(index, source, target):
        def body(k, carry):
            peer = y_peer(k)
            pltpu.make_async_remote_copy(
                src_ref=source(peer), dst_ref=target(y), send_sem=ssem.at[index], recv_sem=rsem.at[index],
                device_id={"dom": peer * n_zc + zc}, device_id_type=MESH,
            ).start()
            return carry

        lax.fori_loop(1, n_y, body, 0)
        pltpu.make_async_copy(source(y), target(y), rsem.at[index]).start()

    owner = jnp.concatenate([eo[0:1, :], eo[1:2, :]], axis=1)
    local = jnp.concatenate([er[0:1, :], er[1:2, :]], axis=1)
    rows = iota((n_dom, ends), 0)
    turned = ((rows & (n_y - 1)) << lzc) + (rows >> ly)
    match = owner == turned
    match_hot = hot(match)
    before = hot(iota((ends, ends), 0) < iota((ends, ends), 1))
    rank = nn(match_hot, before)
    slot = jnp.sum(jnp.where(match, rank, 0.0), axis=0, keepdims=True)
    place[...] = jnp.broadcast_to(owner.astype(F32) * float(SLOTS) + slot, place.shape)

    def lane_rows(at, value):
        lane = iota((LANES, value.shape[1]), 0)
        part = jnp.where(lane < 16, value >> 5, value & 31)
        return jnp.where(at & (lane < 32), part.astype(F32), 0.0).astype(BF)

    wanted = lane_rows(slot == (iota((LANES, ends), 0) & 15).astype(F32), local)
    lane = iota((LANES, n_dom), 0) & 15
    halo_ids = jnp.where(lane == SLOTS, hr[0:1, :], hr[1:2, :])
    halo_wanted = lane_rows((lane == SLOTS) | (lane == SLOTS + 1), halo_ids)
    prow, pcol = iota((n_dom, n_dom), 0), iota((n_dom, n_dom), 1)
    to_zc_y = hot(pcol == ((prow & (n_y - 1)) << lzc) + (prow >> ly))
    to_y_zc = hot(pcol == ((prow & (n_zc - 1)) << ly) + (prow >> lzc))
    requests = nt(match_hot, wanted) + nt(to_zc_y, halo_wanted)
    ids_s[...] = requests.astype(BF).reshape(n_zc, n_y, LANES)

    pl.semaphore_wait(barrier, (n_zc - 1) + (n_y - 1) + (n_x - 1))
    along_zc(0, lambda p: ids_s.at[p], lambda m: ids_r1.at[m])

    tile = min(256, nodes)
    loads[0].wait()
    loads[1].wait()

    @pl.loop(0, nodes // tile)
    def _(i):
        at = pl.ds(pl.multiple_of(i * tile, tile), tile)
        inner[at, :] = nn(adji[at, :], feats[...])

    copies(ids_r1, rsem.at[0]).wait()
    ids_t[...] = nn(to_y_zc, ids_r1[...].reshape(n_dom, LANES)).astype(BF).reshape(n_y, n_zc, LANES)
    along_y(1, lambda p: ids_t.at[p], lambda m: ids_r2.at[m])

    loads[2].wait()
    loads[3].wait()

    @pl.loop(0, nodes // tile)
    def _(i):
        at = pl.ds(pl.multiple_of(i * tile, tile), tile)
        selfp[at, :] = nn(feats[at, :], wself[...]) + b_enc[...]

    ko, jo = iota((halos, halos), 0), iota((halos, halos), 1)
    std = ((((jo >> (lzc + 1)) << lzc) + (jo & (n_zc - 1))) << 1) + ((jo >> lzc) & 1)
    adjp[...] = nn(adjh[...], hot(ko == std)).astype(BF)

    for i in (4, 5, 6):
        loads[i].wait()

    place_col = column_of(place[0:1, :])
    etile = min(256, ends)
    for i in range(ends // etile):
        hot_e[i * etile : (i + 1) * etile, :] = hot(
            place_col[i * etile : (i + 1) * etile, :] == iota((etile, slots), 1).astype(F32)
        )

    copies(ids_r2, rsem.at[1]).wait()
    asked = nn(to_zc_y, ids_r2[...].reshape(n_dom, LANES))
    for c in range(2):
        at = SLOTS + c
        asked_c = 32.0 * asked[:, at : at + 1] + asked[:, at + 16 : at + 17]
        pick = hot(asked_c == iota((n_dom, nodes), 1).astype(F32))
        hal_s[:, c] = nn(pick, hist[...]).astype(BF).reshape(n_zc, n_y, width)
    along_zc(2, lambda p: hal_s.at[p], lambda m: hal_r1.at[m])

    gtile = min(256, slots)
    per = gtile // SLOTS
    id_rows = []
    for i in range(slots // gtile):
        asked = ids_r2[...].reshape(n_dom, LANES)[i * per : (i + 1) * per].astype(F32)
        spread = jnp.broadcast_to(asked[:, None, :], (per, SLOTS, LANES)).reshape(gtile, LANES)
        lane, mine = iota((gtile, LANES), 1), iota((gtile, LANES), 0) & (SLOTS - 1)
        weight = jnp.where(lane == mine, 32.0, jnp.where(lane == mine + 16, 1.0, 0.0))
        id_col = jnp.sum(spread * weight, axis=1, keepdims=True)
        hot_g[i * gtile : (i + 1) * gtile, :] = hot(id_col == iota((gtile, nodes), 1).astype(F32))
        id_rows.append(row_of(id_col))
    id_row = jnp.concatenate(id_rows, axis=1)

    copies(hal_r1, rsem.at[2]).wait()
    io, oo = iota((halos, halos), 1), iota((halos, halos), 0)
    into = ((oo & (n_zc - 1)) << (ly + 1)) + (((oo >> lzc) & 1) << ly) + (oo >> (lzc + 1))
    hal_t[...] = nn(hot(io == into), hal_r1[...].reshape(halos, width)).astype(BF).reshape(n_y, 2 * n_zc, width)
    along_y(3, lambda p: hal_t.at[p], lambda m: hal_r2.at[m])

    @pl.loop(0, nodes // tile)
    def _(i):
        at = pl.ds(pl.multiple_of(i * tile, tile), tile)
        hot_gt[at, :] = hot((iota((tile, slots), 0) + i * tile).astype(F32) == id_row)

    @pl.loop(0, slots // gtile)
    def _(i):
        at = pl.ds(pl.multiple_of(i * gtile, gtile), gtile)
        hot_et[at, :] = hot((iota((gtile, ends), 0) + i * gtile).astype(F32) == place[0:1, :])

    target = column_of(lab[...].astype(F32))

    copies(hal_r2, rsem.at[3]).wait()

    @pl.loop(0, nodes // tile)
    def _(i):
        at = pl.ds(pl.multiple_of(i * tile, tile), tile)
        agg = (inner[at, :] + nn(adjp[at, :], hal_r2[...].reshape(halos, width))).astype(BF)
        emb_o[at, :] = jnp.maximum(selfp[at, :] + nn(agg, wnbr[...]), 0.0).astype(BF)

    @pl.loop(0, slots // gtile)
    def _(i):
        at = pl.ds(pl.multiple_of(i * gtile, gtile), gtile)
        block = nn(hot_g[at, :], emb_o[...]).astype(BF)
        fet_s[pl.ds(i * per, per)] = block.reshape(per, SLOTS, width)

    left, right = pl.ds(0, half), pl.ds(half, half)

    def both_ways(base, send, mid_a, mid_b, recv):
        send4 = send.reshape(n_y, n_zc, SLOTS, width)
        along_zc(base, lambda p: send4.at[:, p, :, left], lambda m: mid_a.at[m])
        along_y(base + 1, lambda p: send4.at[p, :, :, right], lambda m: mid_b.at[m])

    def both_ways_on(base, mid_a, mid_b, recv):
        copies(mid_a, rsem.at[base]).wait()
        along_y(base + 2, lambda p: mid_a.at[:, p], lambda m: recv.at[0, m])
        copies(mid_b, rsem.at[base + 1]).wait()
        along_zc(base + 3, lambda p: mid_b.at[:, p], lambda m: recv.at[1, :, m])

    both_ways(4, fet_s, fet_a, fet_b, fet_r)
    both_ways_on(4, fet_a, fet_b, fet_r)
    copies(fet_r.at[0], rsem.at[6]).wait()
    copies(fet_r.at[1], rsem.at[7]).wait()

    both = [nn(hot_e[...], fet_r[h].reshape(slots, half)) for h in range(2)]
    head = jnp.concatenate([part[:queries] for part in both], axis=1)
    tail = jnp.concatenate([part[queries:] for part in both], axis=1)
    zprod = (head * tail).astype(BF)
    pre = nn(zprod, wdec1[...]) + b_dec1[...]
    sig = jax.nn.sigmoid(pre)
    hidden = (pre * sig).astype(BF).astype(F32)
    wout = w_dec2[...].astype(F32)
    logit = jnp.sum(hidden * wout, axis=1, keepdims=True)
    dlogit = jax.nn.sigmoid(logit) - target
    d_pre = (dlogit * wout * (sig * (1.0 + pre * (1.0 - sig)))).astype(BF)
    dz = nt(d_pre, wdec1[...])
    gpair[:queries, :] = (dz * tail).astype(BF)
    gpair[queries:, :] = (dz * head).astype(BF)

    @pl.loop(0, slots // gtile)
    def _(i):
        at = pl.ds(pl.multiple_of(i * gtile, gtile), gtile)
        block = nn(hot_et[at, :], gpair[...]).astype(BF)
        gra_s[pl.ds(i * per, per)] = block.reshape(per, SLOTS, width)

    both_ways(8, gra_s, gra_a, gra_b, gra_r)

    grad1 = tn(zprod, d_pre)
    gb1 = jnp.sum(d_pre.astype(F32), axis=0, keepdims=True)
    gd2 = jnp.sum(hidden * dlogit, axis=0, keepdims=True)
    vrow = iota((8, width), 0)
    vecs = jnp.where(vrow == 0, gb1, jnp.where(vrow == 1, gd2, 0.0))
    crows = width // 2
    zrows = crows // n_z
    for h in range(2):
        dc_s[h, :crows] = grad1[h * crows : (h + 1) * crows]
        dc_s[h, crows:] = vecs
    other = 1 - core
    pair = pltpu.make_async_remote_copy(
        src_ref=dc_s.at[other], dst_ref=dc_r, send_sem=ssem.at[12], recv_sem=rsem.at[12],
        device_id={"dom": y * n_zc + 2 * z + other}, device_id_type=MESH,
    )
    pair.start()

    def along_z(index, source, goal):
        def body(k, carry):
            peer = lax.rem(z + k, n_z)
            pltpu.make_async_remote_copy(
                src_ref=source(peer), dst_ref=goal(z), send_sem=ssem.at[index], recv_sem=rsem.at[index],
                device_id={"dom": y * n_zc + 2 * peer + core}, device_id_type=MESH,
            ).start()
            return carry

        lax.fori_loop(1, n_z, body, 0)
        pltpu.make_async_copy(source(z), goal(z), rsem.at[index]).start()

    pair.wait_recv()
    for j in range(n_z):
        dz_s[j, :zrows] = dc_s[core, j * zrows : (j + 1) * zrows] + dc_r[j * zrows : (j + 1) * zrows]
        dz_s[j, zrows:] = dc_s[core, crows:] + dc_r[crows:]
    along_z(13, lambda p: dz_s.at[p], lambda m: dz_r.at[m])

    both_ways_on(8, gra_a, gra_b, gra_r)

    copies(dz_r, rsem.at[13]).wait()
    total = dz_r[0]
    for j in range(1, n_z):
        total = total + dz_r[j]
    zbuf[...] = total
    along_y(14, lambda p: zbuf, lambda m: dy_r.at[m])

    copies(dy_r, rsem.at[14]).wait()
    total = dy_r[0]
    for j in range(1, n_y):
        total = total + dy_r[j]
    dbuf[...] = total
    for k in range(1, n_x):
        pltpu.make_async_remote_copy(
            src_ref=dbuf, dst_ref=dx_r.at[rep], send_sem=ssem.at[15], recv_sem=rsem.at[15],
            device_id={"rep": lax.rem(rep + k, n_x)}, device_id_type=MESH,
        ).start()
    pltpu.make_async_copy(dbuf, dx_r.at[rep], rsem.at[15]).start()

    flip = rep + 1 - 2 * lax.rem(rep, 2)
    wrap = 3 - rep
    wflip = wrap + 1 - 2 * lax.rem(wrap, 2)
    quarter = nodes // n_x
    jtile = min(64, quarter)

    def local_sum(q, cols):
        at = pl.ds(pl.multiple_of(q * quarter, quarter), quarter)
        return nn(hot_gt[at, :], gra_r[cols].reshape(slots, half))

    def trade(index, source, goal, partner):
        copy = pltpu.make_async_remote_copy(
            src_ref=source, dst_ref=goal, send_sem=ssem.at[index], recv_sem=rsem.at[index],
            device_id={"rep": partner}, device_id_type=MESH,
        )
        copy.start()
        return copy

    def joined(way, part):
        @pl.loop(0, quarter // jtile)
        def _(i):
            at = pl.ds(pl.multiple_of(i * jtile, jtile), jtile)
            xs2[way, at, :] = (xk[part, at, :] + xr1[way, 1, at, :].astype(F32)).astype(BF)

    copies(gra_r.at[0], rsem.at[10]).wait()
    xs1[0, 0] = local_sum(flip, 0).astype(BF)
    xs1[0, 1] = local_sum(wflip, 0).astype(BF)
    one = trade(16, xs1.at[0], xr1.at[0], flip)
    copies(gra_r.at[1], rsem.at[11]).wait()
    xs1[1, 0] = local_sum(wrap, 1).astype(BF)
    xs1[1, 1] = local_sum(wflip, 1).astype(BF)
    two = trade(17, xs1.at[1], xr1.at[1], wrap)
    xk[0] = local_sum(rep, 0)
    xk[1] = local_sum(rep, 1)
    xk[2] = local_sum(wrap, 0)
    xk[3] = local_sum(flip, 1)
    one.wait_recv()
    joined(0, 2)
    three = trade(18, xs2.at[0], xr2.at[0], wrap)
    two.wait_recv()
    joined(1, 3)
    four = trade(19, xs2.at[1], xr2.at[1], flip)

    copies(dx_r, rsem.at[15]).wait()
    total = dx_r[0]
    for j in range(1, n_x):
        total = total + dx_r[j]
    zbuf2 = total[:zrows]
    gv_o[...] = total[zrows:]
    dc_r[:zrows] = zbuf2
    along_z(20, lambda p: dc_r.at[pl.ds(0, zrows)], lambda m: dg_r.at[core, m])

    three.wait_recv()
    ge_o[:, :half] = xk[0] + xr1[0, 0].astype(F32) + xr2[0].astype(F32)
    four.wait_recv()
    ge_o[:, half:] = xk[1] + xr1[1, 0].astype(F32) + xr2[1].astype(F32)

    copies(dg_r.at[0], rsem.at[20]).wait()
    last = pltpu.make_async_remote_copy(
        src_ref=dg_r.at[core], dst_ref=dg_r.at[core], send_sem=ssem.at[21], recv_sem=rsem.at[21],
        device_id={"dom": y * n_zc + 2 * z + other}, device_id_type=MESH,
    )
    last.start()

    copies(ids_s.at[pl.ds(0, n_zc - 1)], ssem.at[0]).wait()
    copies(ids_t.at[pl.ds(0, n_y - 1)], ssem.at[1]).wait()
    copies(hal_s.at[pl.ds(0, n_zc - 1)], ssem.at[2]).wait()
    copies(hal_t.at[pl.ds(0, n_y - 1)], ssem.at[3]).wait()
    for base, mid_a, mid_b in ((4, fet_a, fet_b), (8, gra_a, gra_b)):
        copies(mid_a.at[pl.ds(0, n_zc - 1)], ssem.at[base]).wait()
        copies(mid_b.at[pl.ds(0, n_y - 1)], ssem.at[base + 1]).wait()
        copies(mid_b.at[pl.ds(0, n_y - 1)], ssem.at[base + 2]).wait()
        copies(mid_a.at[pl.ds(0, n_zc - 1)], ssem.at[base + 3]).wait()
    pair.wait_send()
    copies(dz_s.at[pl.ds(0, n_z - 1)], ssem.at[13]).wait()
    copies(dy_r.at[pl.ds(0, n_y - 1)], ssem.at[14]).wait()
    copies(dx_r.at[pl.ds(0, n_x - 1)], ssem.at[15]).wait()
    for copy in (one, two, three, four):
        copy.wait_send()
    copies(dg_r.at[0, pl.ds(0, n_z - 1)], ssem.at[20]).wait()
    last.wait()
    gd_o[...] = dg_r[...].reshape(width, width)


def per_device(
    feats, history, adj_inner, adj_halo, halo_rows, w_self, w_nbr, b_enc,
    edge_owner, edge_rows, labels, w_dec1, b_dec1, w_dec2,
):
    n_dom, n_x = lax.axis_size("dom"), lax.axis_size("rep")
    n_zc = 16 if n_dom == 128 else 4
    n_y = n_dom // n_zc
    nodes, width = feats.shape
    halos = adj_halo.shape[1]
    queries = edge_owner.shape[0]
    ends = 2 * queries
    slots = n_dom * SLOTS
    half = width // 2
    n_z = n_zc // 2
    quarter = nodes // n_x
    crows = width // 2
    zrows = crows // n_z
    vmem = pl.BlockSpec(memory_space=pltpu.VMEM)
    any_ = pl.BlockSpec(memory_space=pl.ANY)
    V = pltpu.VMEM
    outs = pl.pallas_call(
        functools.partial(kernel, n_y, n_zc, n_x),
        out_shape=(
            jax.ShapeDtypeStruct((nodes, width), BF),
            jax.ShapeDtypeStruct((quarter, width), F32),
            jax.ShapeDtypeStruct((width, width), F32),
            jax.ShapeDtypeStruct((8, width), F32),
        ),
        in_specs=[vmem] * 7 + [any_] * 7,
        out_specs=(vmem,) * 4,
        scratch_shapes=[
            V((nodes, width), BF), V((nodes, width), BF), V((nodes, nodes), BF), V((nodes, halos), BF),
            V((width, width), BF), V((width, width), BF), V((width, width), BF),
            V((n_zc, n_y, LANES), BF), V((n_zc, n_y, LANES), BF), V((n_y, n_zc, LANES), BF), V((n_y, n_zc, LANES), BF),
            V((n_zc, 2, n_y, width), BF), V((n_zc, 2, n_y, width), BF), V((n_y, 2 * n_zc, width), BF),
            V((n_y, 2 * n_zc, width), BF), V((nodes, halos), BF),
            V((nodes, width), F32), V((nodes, width), F32), V((8, ends), F32),
            V((ends, slots), BF), V((slots, ends), BF), V((slots, nodes), BF), V((nodes, slots), BF),
            V((n_dom, SLOTS, width), BF), V((n_zc, n_y, SLOTS, half), BF), V((n_y, n_zc, SLOTS, half), BF),
            V((2, n_y, n_zc, SLOTS, half), BF),
            V((n_dom, SLOTS, width), BF), V((n_zc, n_y, SLOTS, half), BF), V((n_y, n_zc, SLOTS, half), BF),
            V((2, n_y, n_zc, SLOTS, half), BF), V((ends, width), BF),
            V((zrows + 8, width), F32), V((zrows + 8, width), F32),
            V((2, 2, quarter, half), BF), V((2, 2, quarter, half), BF), V((2, quarter, half), BF),
            V((2, quarter, half), BF), V((4, quarter, half), F32),
            V((2, crows + 8, width), F32), V((crows + 8, width), F32),
            V((n_z, zrows + 8, width), F32), V((n_z, zrows + 8, width), F32),
            V((n_y, zrows + 8, width), F32), V((n_x, zrows + 8, width), F32), V((2, n_z, zrows, width), F32),
            pltpu.SemaphoreType.DMA((7,)), pltpu.SemaphoreType.DMA((4,)),
            pltpu.SemaphoreType.DMA((22,)), pltpu.SemaphoreType.DMA((22,)),
        ],
        compiler_params=pltpu.CompilerParams(
            collective_id=0, has_side_effects=True, vmem_limit_bytes=60 * 1024 * 1024
        ),
        name="encode_decode",
    )(
        edge_owner.T, edge_rows.T, halo_rows.T, labels.reshape(1, -1), b_enc.reshape(1, -1), b_dec1.reshape(1, -1),
        w_dec2.reshape(1, -1), feats, history, adj_inner, adj_halo, w_self, w_nbr, w_dec1,
    )
    embed, grad_embed, grad_dec1, vecs = outs
    return embed, grad_embed, grad_dec1, vecs[0], vecs[1]


def solution(mesh):
    placed = (
        P("dom", None), P("dom", None), P("dom", None), P("dom", None), P("dom", None), P(), P(), P(),
        P(("dom", "rep"), None), P(("dom", "rep"), None), P(("dom", "rep")), P(), P(), P(),
    )
    return jax.shard_map(
        per_device,
        mesh=mesh,
        in_specs=placed,
        out_specs=(P("dom", None), P(("dom", "rep"), None), P(), P(), P()),
        check_vma=False,
    )
```

time: 415 us -> 107 us (0.26)
  waiting for transfers between devices: 212 us -> 0 us
  Pallas kernels: 0 us -> 97.9 us
  blocking collectives: 97.7 us -> 0 us
  starting transfers between devices: 49.3 us -> 0 us
  between operations: 15.9 us -> 0.64 us
  local copies, waits for them, and re-layouts: 22.4 us -> 7.77 us
  other arithmetic: 9.45 us -> 0 us
  matrix products: 6.73 us -> 0 us
    psum x1 -> x0, waiting for transfers between devices: 141 us -> none  [per_device(): grad_dec1, grad_bias1, grad_dec2 = lax.psum((gw1, gb1, gw2), ('dom', 'rep'))]
    pallas_call x0 -> x1, Pallas kernels: none -> 97.9 us  [per_device(): pl.pallas_call(functools.partial(kernel, n_y, n_zc, n_x), out_shape=(jax....]
    psum x1 -> x0, blocking collectives: 97.7 us -> none  [per_device(): grad_dec1, grad_bias1, grad_dec2 = lax.psum((gw1, gb1, gw2), ('dom', 'rep'))]
    all_to_all x5 -> x0, waiting for transfers between devices: 71.1 us -> none  [the longest x1 27.9 us: per_device(): lax.all_to_all(send_grads.reshape(n_dom, cap_edge, width), 'dom', split_a...]
    all_to_all x5 -> x0, starting transfers between devices: 49.3 us -> none  [the longest x1 18.4 us: per_device(): lax.all_to_all(halo_rows, 'dom', split_axis=0, concat_axis=0, tiled=True)]
    gather x4 -> x0, local copies, waits for them, and re-layouts: 8.77 us -> none  [the longest x1 4.96 us: per_device(): embed[wanted]]
    scatter-add x1 -> x0, other arithmetic: 7.12 us -> none  [per_device(): jnp.zeros((nodes, width), jnp.float32).at[wanted.reshape(-1)]]
    dot_general x7 -> x0, matrix products: 6.73 us -> none  [the longest x1 2.17 us: encode_block(): jnp.dot(agg, w_nbr, preferred_element_type=jnp.float32)]
  transfers between devices with their start and end apart: 7 -> 0, of which waited for: 6 -> 0; matrix products, arithmetic and copies ran while one was open for 5% -> 0% of each run, Pallas kernels for 0% -> 0%
where the time goes in v1:
time: 107 us; the launch traced here: 106 us
  Pallas kernels  97.9 us (91%)
  local copies, waits for them, and re-layouts  7.77 us (7%)
    pallas_call x1, Pallas kernels, per_device(): pl.pallas_call(functools.partial(kernel, n_y, n_zc, n_x), out_shape=(jax....  97.9 us
    unnamed x3, local copies, waits for them, and re-layouts  5.2 us

profile of v1, /device:TPU:1, one launch (start us, length us, event | category | flops | bytes accessed | tf_op | source)
XLA Modules:
  0.0 106.4 jit_solution(6791535642645752974)
XLA Ops:
  0.6 1.2 %reshape.25.w_dec2 = bf16[1,256]{1,0:T(2,128)(2,1)} reshape(bf16[256]{0:T(256)(128)(2,1)} %param.27) | data formatting | bytes 1024 | tf_op jit(solution)/shard_map/reshape | solution.py:500
  1.9 97.9 %encode_decode.1 = (bf16[1024,256]{1,0:T(8,128)(2,1)}, f32[256,256]{1,0:T(8,128)}, f32[256,256]{1,0:T(8,128)}, f32[8,256]{1,0:T(8,128)}) custom-call(s32[2,256]{1,0:T(2,128)} %bitcast.8, s32[2,256]{1,0:T(2,128)} %bitcast.9, s32[2,128]{1,0:T(2,128)} %bitcast.10, s32[1,256]{1,0:T(1,128)} %bitcast.11, f32[1,256]{1,0:T(1,128)} %bitcast.12, f32[1,256]{1,0:T(1,128)} %bitcast.13, ...), custom_call_target="tpu_custom_call" | custom-call | tf_op jit(solution)/shard_map/encode_decode/pallas_call | solution.py:463
  99.8 1.3 %fusion = (f32[1,256]{1,0:T(1,128)}, f32[1,256]{1,0:T(1,128)}) fusion(f32[8,256]{1,0:T(8,128)} %get-tuple-element.12), kind=kLoop, calls=%fused_computation | loop fusion | bytes 4096 | tf_op jit(solution)/shard_map/slice | solution.py:503
  101.1 1.9 %copy.22 = bf16[1024,256]{1,0:T(8,128)(2,1)} copy(bf16[1024,256]{1,0:T(8,128)(2,1)} %get-tuple-element.20) | data formatting | bytes 1048576
  103.0 1.7 %copy.23 = f32[256,256]{1,0:T(8,128)} copy(f32[256,256]{1,0:T(8,128)} %get-tuple-element.21) | data formatting | bytes 524288
  104.7 1.7 %copy.24 = f32[256,256]{1,0:T(8,128)} copy(f32[256,256]{1,0:T(8,128)} %get-tuple-element.22) | data formatting | bytes 524288

commit v2 on v1

--- a/solution.py
+++ b/solution.py
@@ -117,7 +117,13 @@
     for k in range(1, n_x):
         pl.semaphore_signal(barrier, inc=1, device_id={"rep": lax.rem(rep + k, n_x)}, device_id_type=MESH)
 
-    def along_zc(index, source, target):
+    sent = []
+
+    def drain():
+        for index, size in sent:
+            copies(size, ssem.at[index]).wait()
+
+    def along_zc(index, source, target, sent_size):
         def body(k, carry):
             peer = zc_peer(k)
             pltpu.make_async_remote_copy(
@@ -128,8 +134,9 @@
 
         lax.fori_loop(1, n_zc, body, 0)
         pltpu.make_async_copy(source(zc), target(zc), rsem.at[index]).start()
-
-    def along_y(index, source, target):
+        sent.append((index, sent_size))
+
+    def along_y(index, source, target, sent_size):
         def body(k, carry):
             peer = y_peer(k)
             pltpu.make_async_remote_copy(
@@ -140,6 +147,7 @@
 
         lax.fori_loop(1, n_y, body, 0)
         pltpu.make_async_copy(source(y), target(y), rsem.at[index]).start()
+        sent.append((index, sent_size))
 
     owner = jnp.concatenate([eo[0:1, :], eo[1:2, :]], axis=1)
     local = jnp.concatenate([er[0:1, :], er[1:2, :]], axis=1)
@@ -168,7 +176,7 @@
     ids_s[...] = requests.astype(BF).reshape(n_zc, n_y, LANES)
 
     pl.semaphore_wait(barrier, (n_zc - 1) + (n_y - 1) + (n_x - 1))
-    along_zc(0, lambda p: ids_s.at[p], lambda m: ids_r1.at[m])
+    along_zc(0, lambda p: ids_s.at[p], lambda m: ids_r1.at[m], ids_s.at[pl.ds(0, n_zc - 1)])
 
     tile = min(256, nodes)
     loads[0].wait()
@@ -181,7 +189,7 @@
 
     copies(ids_r1, rsem.at[0]).wait()
     ids_t[...] = nn(to_y_zc, ids_r1[...].reshape(n_dom, LANES)).astype(BF).reshape(n_y, n_zc, LANES)
-    along_y(1, lambda p: ids_t.at[p], lambda m: ids_r2.at[m])
+    along_y(1, lambda p: ids_t.at[p], lambda m: ids_r2.at[m], ids_t.at[pl.ds(0, n_y - 1)])
 
     loads[2].wait()
     loads[3].wait()
@@ -212,7 +220,7 @@
         asked_c = 32.0 * asked[:, at : at + 1] + asked[:, at + 16 : at + 17]
         pick = hot(asked_c == iota((n_dom, nodes), 1).astype(F32))
         hal_s[:, c] = nn(pick, hist[...]).astype(BF).reshape(n_zc, n_y, width)
-    along_zc(2, lambda p: hal_s.at[p], lambda m: hal_r1.at[m])
+    along_zc(2, lambda p: hal_s.at[p], lambda m: hal_r1.at[m], hal_s.at[pl.ds(0, n_zc - 1)])
 
     gtile = min(256, slots)
     per = gtile // SLOTS
@@ -231,7 +239,7 @@
     io, oo = iota((halos, halos), 1), iota((halos, halos), 0)
     into = ((oo & (n_zc - 1)) << (ly + 1)) + (((oo >> lzc) & 1) << ly) + (oo >> (lzc + 1))
     hal_t[...] = nn(hot(io == into), hal_r1[...].reshape(halos, width)).astype(BF).reshape(n_y, 2 * n_zc, width)
-    along_y(3, lambda p: hal_t.at[p], lambda m: hal_r2.at[m])
+    along_y(3, lambda p: hal_t.at[p], lambda m: hal_r2.at[m], hal_t.at[pl.ds(0, n_y - 1)])
 
     @pl.loop(0, nodes // tile)
     def _(i):
@@ -263,14 +271,14 @@
 
     def both_ways(base, send, mid_a, mid_b, recv):
         send4 = send.reshape(n_y, n_zc, SLOTS, width)
-        along_zc(base, lambda p: send4.at[:, p, :, left], lambda m: mid_a.at[m])
-        along_y(base + 1, lambda p: send4.at[p, :, :, right], lambda m: mid_b.at[m])
+        along_zc(base, lambda p: send4.at[:, p, :, left], lambda m: mid_a.at[m], mid_a.at[pl.ds(0, n_zc - 1)])
+        along_y(base + 1, lambda p: send4.at[p, :, :, right], lambda m: mid_b.at[m], mid_b.at[pl.ds(0, n_y - 1)])
 
     def both_ways_on(base, mid_a, mid_b, recv):
         copies(mid_a, rsem.at[base]).wait()
-        along_y(base + 2, lambda p: mid_a.at[:, p], lambda m: recv.at[0, m])
+        along_y(base + 2, lambda p: mid_a.at[:, p], lambda m: recv.at[0, m], mid_b.at[pl.ds(0, n_y - 1)])
         copies(mid_b, rsem.at[base + 1]).wait()
-        along_zc(base + 3, lambda p: mid_b.at[:, p], lambda m: recv.at[1, :, m])
+        along_zc(base + 3, lambda p: mid_b.at[:, p], lambda m: recv.at[1, :, m], mid_a.at[pl.ds(0, n_zc - 1)])
 
     both_ways(4, fet_s, fet_a, fet_b, fet_r)
     both_ways_on(4, fet_a, fet_b, fet_r)
@@ -284,7 +292,7 @@
     pre = nn(zprod, wdec1[...]) + b_dec1[...]
     sig = jax.nn.sigmoid(pre)
     hidden = (pre * sig).astype(BF).astype(F32)
-    wout = w_dec2[...].astype(F32)
+    wout = w_dec2[...].astype(F32).reshape(1, width)
     logit = jnp.sum(hidden * wout, axis=1, keepdims=True)
     dlogit = jax.nn.sigmoid(logit) - target
     d_pre = (dlogit * wout * (sig * (1.0 + pre * (1.0 - sig)))).astype(BF)
@@ -317,7 +325,7 @@
     )
     pair.start()
 
-    def along_z(index, source, goal):
+    def along_z(index, source, goal, sent_size):
         def body(k, carry):
             peer = lax.rem(z + k, n_z)
             pltpu.make_async_remote_copy(
@@ -328,12 +336,13 @@
 
         lax.fori_loop(1, n_z, body, 0)
         pltpu.make_async_copy(source(z), goal(z), rsem.at[index]).start()
+        sent.append((index, sent_size))
 
     pair.wait_recv()
     for j in range(n_z):
         dz_s[j, :zrows] = dc_s[core, j * zrows : (j + 1) * zrows] + dc_r[j * zrows : (j + 1) * zrows]
         dz_s[j, zrows:] = dc_s[core, crows:] + dc_r[crows:]
-    along_z(13, lambda p: dz_s.at[p], lambda m: dz_r.at[m])
+    along_z(13, lambda p: dz_s.at[p], lambda m: dz_r.at[m], dz_s.at[pl.ds(0, n_z - 1)])
 
     both_ways_on(8, gra_a, gra_b, gra_r)
 
@@ -342,7 +351,7 @@
     for j in range(1, n_z):
         total = total + dz_r[j]
     zbuf[...] = total
-    along_y(14, lambda p: zbuf, lambda m: dy_r.at[m])
+    along_y(14, lambda p: zbuf, lambda m: dy_r.at[m], dy_r.at[pl.ds(0, n_y - 1)])
 
     copies(dy_r, rsem.at[14]).wait()
     total = dy_r[0]
@@ -355,6 +364,7 @@
             device_id={"rep": lax.rem(rep + k, n_x)}, device_id_type=MESH,
         ).start()
     pltpu.make_async_copy(dbuf, dx_r.at[rep], rsem.at[15]).start()
+    sent.append((15, dx_r.at[pl.ds(0, n_x - 1)]))
 
     flip = rep + 1 - 2 * lax.rem(rep, 2)
     wrap = 3 - rep
@@ -406,7 +416,7 @@
     zbuf2 = total[:zrows]
     gv_o[...] = total[zrows:]
     dc_r[:zrows] = zbuf2
-    along_z(20, lambda p: dc_r.at[pl.ds(0, zrows)], lambda m: dg_r.at[core, m])
+    along_z(20, lambda p: dc_r.at[pl.ds(0, zrows)], lambda m: dg_r.at[core, m], dg_r.at[0, pl.ds(0, n_z - 1)])
 
     three.wait_recv()
     ge_o[:, :half] = xk[0] + xr1[0, 0].astype(F32) + xr2[0].astype(F32)
@@ -420,24 +430,21 @@
     )
     last.start()
 
-    copies(ids_s.at[pl.ds(0, n_zc - 1)], ssem.at[0]).wait()
-    copies(ids_t.at[pl.ds(0, n_y - 1)], ssem.at[1]).wait()
-    copies(hal_s.at[pl.ds(0, n_zc - 1)], ssem.at[2]).wait()
-    copies(hal_t.at[pl.ds(0, n_y - 1)], ssem.at[3]).wait()
-    for base, mid_a, mid_b in ((4, fet_a, fet_b), (8, gra_a, gra_b)):
-        copies(mid_a.at[pl.ds(0, n_zc - 1)], ssem.at[base]).wait()
-        copies(mid_b.at[pl.ds(0, n_y - 1)], ssem.at[base + 1]).wait()
-        copies(mid_b.at[pl.ds(0, n_y - 1)], ssem.at[base + 2]).wait()
-        copies(mid_a.at[pl.ds(0, n_zc - 1)], ssem.at[base + 3]).wait()
+    drain()
     pair.wait_send()
-    copies(dz_s.at[pl.ds(0, n_z - 1)], ssem.at[13]).wait()
-    copies(dy_r.at[pl.ds(0, n_y - 1)], ssem.at[14]).wait()
-    copies(dx_r.at[pl.ds(0, n_x - 1)], ssem.at[15]).wait()
     for copy in (one, two, three, four):
         copy.wait_send()
-    copies(dg_r.at[0, pl.ds(0, n_z - 1)], ssem.at[20]).wait()
     last.wait()
     gd_o[...] = dg_r[...].reshape(width, width)
+
+
+def put_out(emb, ge, gd, gv, emb_h, ge_h, gd_h, gb_h, g2_h, sem):
+    pairs = ((emb, emb_h), (ge, ge_h), (gd, gd_h), (gv.at[pl.ds(0, 1)], gb_h), (gv.at[pl.ds(1, 1)], g2_h))
+    copies_out = [pltpu.make_async_copy(src, dst, sem.at[i]) for i, (src, dst) in enumerate(pairs)]
+    for copy in copies_out:
+        copy.start()
+    for copy in copies_out:
+        copy.wait()
 
 
 def per_device(
@@ -463,10 +470,10 @@
     outs = pl.pallas_call(
         functools.partial(kernel, n_y, n_zc, n_x),
         out_shape=(
-            jax.ShapeDtypeStruct((nodes, width), BF),
-            jax.ShapeDtypeStruct((quarter, width), F32),
-            jax.ShapeDtypeStruct((width, width), F32),
-            jax.ShapeDtypeStruct((8, width), F32),
+            V((nodes, width), BF),
+            V((quarter, width), F32),
+            V((width, width), F32),
+            V((8, width), F32),
         ),
         in_specs=[vmem] * 7 + [any_] * 7,
         out_specs=(vmem,) * 4,
@@ -497,10 +504,18 @@
         name="encode_decode",
     )(
         edge_owner.T, edge_rows.T, halo_rows.T, labels.reshape(1, -1), b_enc.reshape(1, -1), b_dec1.reshape(1, -1),
-        w_dec2.reshape(1, -1), feats, history, adj_inner, adj_halo, w_self, w_nbr, w_dec1,
+        w_dec2, feats, history, adj_inner, adj_halo, w_self, w_nbr, w_dec1,
     )
-    embed, grad_embed, grad_dec1, vecs = outs
-    return embed, grad_embed, grad_dec1, vecs[0], vecs[1]
+    shapes = ((nodes, width, BF), (quarter, width, F32), (width, width, F32), (1, width, F32), (1, width, F32))
+    embed, grad_embed, grad_dec1, bias1, dec2 = pl.pallas_call(
+        put_out,
+        out_shape=tuple(jax.ShapeDtypeStruct(shape[:2], shape[2]) for shape in shapes),
+        in_specs=[vmem] * 4,
+        out_specs=(any_,) * 5,
+        scratch_shapes=[pltpu.SemaphoreType.DMA((5,))],
+        name="put_out",
+    )(*[pltpu.with_memory_space_constraint(out, pltpu.VMEM) for out in outs])
+    return embed, grad_embed, grad_dec1, bias1.reshape(-1), dec2.reshape(-1)
 
 
 def solution(mesh):

time: 107 us -> 98.5 us (0.921)
  local copies, waits for them, and re-layouts: 7.77 us -> 0 us
    unnamed x3 -> x0, local copies, waits for them, and re-layouts: 5.2 us -> none
    slice x1 -> x0, local copies, waits for them, and re-layouts: 1.34 us -> none  [per_device(): return (embed, grad_embed, grad_dec1, vecs[0], vecs[1])]
    reshape x1 -> x0, local copies, waits for them, and re-layouts: 1.22 us -> none  [per_device(): w_dec2.reshape(1, -1)]
    pallas_call x1 -> x2, Pallas kernels: 97.9 us -> 97.7 us  [the longest x1 96.7 us: per_device(): pl.pallas_call(functools.partial(kernel, n_y, n_zc, n_x), out_shape=(V((n...]
where the time goes in v2:
time: 98.5 us; the launch traced here: 98.3 us
  Pallas kernels  97.7 us (99%)
    pallas_call x1, Pallas kernels, per_device(): pl.pallas_call(functools.partial(kernel, n_y, n_zc, n_x), out_shape=(V((n...  96.7 us

profile of v2, /device:TPU:1, one launch (start us, length us, event | category | flops | bytes accessed | tf_op | source)
XLA Modules:
  0.0 98.3 jit_solution(240512551227239750)
XLA Ops:
  0.6 96.7 %encode_decode.1 = (bf16[1024,256]{1,0:T(8,128)(2,1)S(1)}, f32[256,256]{1,0:T(8,128)S(1)}, f32[256,256]{1,0:T(8,128)S(1)}, f32[8,256]{1,0:T(8,128)S(1)}) custom-call(s32[2,256]{1,0:T(2,128)} %bitcast.8, s32[2,256]{1,0:T(2,128)} %bitcast.9, s32[2,128]{1,0:T(2,128)} %bitcast.10, s32[1,256]{1,0:T(1,128)} %bitcast.11, f32[1,256]{1,0:T(1,128)} %bitcast.12, ...), custom_call_target="tpu_custom_call" | custom-call | tf_op jit(solution)/shard_map/encode_decode/pallas_call | solution.py:470
  97.3 1.0 %put_out.1 = (bf16[1024,256]{1,0:T(8,128)(2,1)}, f32[256,256]{1,0:T(8,128)}, f32[256,256]{1,0:T(8,128)}, f32[1,256]{1,0:T(1,128)}, f32[1,256]{1,0:T(1,128)}) custom-call(bf16[1024,256]{1,0:T(8,128)(2,1)S(1)} %get-tuple-element.14.emb, f32[256,256]{1,0:T(8,128)S(1)} %get-tuple-element.15.ge, f32[256,256]{1,0:T(8,128)S(1)} %get-tuple-element.16.gd, ...), custom_call_target="tpu_custom_call" | custom-call | tf_op jit(solution)/shard_map/put_out/pallas_call | solution.py:510

commit v3 on v2

--- a/solution.py
+++ b/solution.py
@@ -60,7 +60,7 @@
     emb_o, ge_o, gd_o, gv_o,
     feats, hist, adji, adjh, wself, wnbr, wdec1,
     ids_s, ids_r1, ids_t, ids_r2,
-    hal_s, hal_r1, hal_t, hal_r2, adjp,
+    hal_s, hal_r1, hal_t, hal_r2, hal_m, hal_u, hal_v, hal_w, halo, adjp,
     inner, selfp, place,
     hot_e, hot_et, hot_g, hot_gt,
     fet_s, fet_a, fet_b, fet_r,
@@ -219,8 +219,15 @@
         at = SLOTS + c
         asked_c = 32.0 * asked[:, at : at + 1] + asked[:, at + 16 : at + 17]
         pick = hot(asked_c == iota((n_dom, nodes), 1).astype(F32))
-        hal_s[:, c] = nn(pick, hist[...]).astype(BF).reshape(n_zc, n_y, width)
+        picked = nn(pick, hist[...]).astype(BF)
+        hal_s[:, c] = picked[:, :half].reshape(n_zc, n_y, half)
+        hal_m[:, c] = picked[:, half:].reshape(n_zc, n_y, half)
     along_zc(2, lambda p: hal_s.at[p], lambda m: hal_r1.at[m], hal_s.at[pl.ds(0, n_zc - 1)])
+    io, oo = iota((halos, halos), 1), iota((halos, halos), 0)
+    turn = hot(io == ((oo & (n_zc - 1)) << (ly + 1)) + (((oo >> lzc) & 1) << ly) + (oo >> (lzc + 1)))
+    back = hot(io == ((oo & (n_y - 1)) << (lzc + 1)) + (((oo >> ly) & 1) << lzc) + (oo >> (ly + 1)))
+    hal_u[...] = nn(turn, hal_m[...].reshape(halos, half)).astype(BF).reshape(n_y, 2 * n_zc, half)
+    along_y(22, lambda p: hal_u.at[p], lambda m: hal_v.at[m], hal_u.at[pl.ds(0, n_y - 1)])
 
     gtile = min(256, slots)
     per = gtile // SLOTS
@@ -236,10 +243,11 @@
     id_row = jnp.concatenate(id_rows, axis=1)
 
     copies(hal_r1, rsem.at[2]).wait()
-    io, oo = iota((halos, halos), 1), iota((halos, halos), 0)
-    into = ((oo & (n_zc - 1)) << (ly + 1)) + (((oo >> lzc) & 1) << ly) + (oo >> (lzc + 1))
-    hal_t[...] = nn(hot(io == into), hal_r1[...].reshape(halos, width)).astype(BF).reshape(n_y, 2 * n_zc, width)
+    hal_t[...] = nn(turn, hal_r1[...].reshape(halos, half)).astype(BF).reshape(n_y, 2 * n_zc, half)
     along_y(3, lambda p: hal_t.at[p], lambda m: hal_r2.at[m], hal_t.at[pl.ds(0, n_y - 1)])
+    copies(hal_v, rsem.at[22]).wait()
+    hal_m[...] = nn(back, hal_v[...].reshape(halos, half)).astype(BF).reshape(n_zc, 2, n_y, half)
+    along_zc(23, lambda p: hal_m.at[p], lambda m: hal_w.at[m], hal_m.at[pl.ds(0, n_zc - 1)])
 
     @pl.loop(0, nodes // tile)
     def _(i):
@@ -254,11 +262,14 @@
     target = column_of(lab[...].astype(F32))
 
     copies(hal_r2, rsem.at[3]).wait()
+    copies(hal_w, rsem.at[23]).wait()
+    halo[:, :half] = hal_r2[...].reshape(halos, half)
+    halo[:, half:] = nn(turn, hal_w[...].reshape(halos, half)).astype(BF)
 
     @pl.loop(0, nodes // tile)
     def _(i):
         at = pl.ds(pl.multiple_of(i * tile, tile), tile)
-        agg = (inner[at, :] + nn(adjp[at, :], hal_r2[...].reshape(halos, width))).astype(BF)
+        agg = (inner[at, :] + nn(adjp[at, :], halo[...])).astype(BF)
         emb_o[at, :] = jnp.maximum(selfp[at, :] + nn(agg, wnbr[...]), 0.0).astype(BF)
 
     @pl.loop(0, slots // gtile)
@@ -276,18 +287,18 @@
 
     def both_ways_on(base, mid_a, mid_b, recv):
         copies(mid_a, rsem.at[base]).wait()
-        along_y(base + 2, lambda p: mid_a.at[:, p], lambda m: recv.at[0, m], mid_b.at[pl.ds(0, n_y - 1)])
+        along_y(base + 2, lambda p: mid_a.at[:, p], lambda m: recv.at[m, :, :, left], mid_b.at[pl.ds(0, n_y - 1)])
         copies(mid_b, rsem.at[base + 1]).wait()
-        along_zc(base + 3, lambda p: mid_b.at[:, p], lambda m: recv.at[1, :, m], mid_a.at[pl.ds(0, n_zc - 1)])
+        along_zc(base + 3, lambda p: mid_b.at[:, p], lambda m: recv.at[:, m, :, right], mid_a.at[pl.ds(0, n_zc - 1)])
 
     both_ways(4, fet_s, fet_a, fet_b, fet_r)
     both_ways_on(4, fet_a, fet_b, fet_r)
-    copies(fet_r.at[0], rsem.at[6]).wait()
-    copies(fet_r.at[1], rsem.at[7]).wait()
-
-    both = [nn(hot_e[...], fet_r[h].reshape(slots, half)) for h in range(2)]
-    head = jnp.concatenate([part[:queries] for part in both], axis=1)
-    tail = jnp.concatenate([part[queries:] for part in both], axis=1)
+    copies(fet_r.at[:, :, :, left], rsem.at[6]).wait()
+    copies(fet_r.at[:, :, :, right], rsem.at[7]).wait()
+
+    got = fet_r[...].reshape(slots, width)
+    head = nn(hot_e[:queries, :], got)
+    tail = nn(hot_e[queries:, :], got)
     zprod = (head * tail).astype(BF)
     pre = nn(zprod, wdec1[...]) + b_dec1[...]
     sig = jax.nn.sigmoid(pre)
@@ -296,18 +307,6 @@
     logit = jnp.sum(hidden * wout, axis=1, keepdims=True)
     dlogit = jax.nn.sigmoid(logit) - target
     d_pre = (dlogit * wout * (sig * (1.0 + pre * (1.0 - sig)))).astype(BF)
-    dz = nt(d_pre, wdec1[...])
-    gpair[:queries, :] = (dz * tail).astype(BF)
-    gpair[queries:, :] = (dz * head).astype(BF)
-
-    @pl.loop(0, slots // gtile)
-    def _(i):
-        at = pl.ds(pl.multiple_of(i * gtile, gtile), gtile)
-        block = nn(hot_et[at, :], gpair[...]).astype(BF)
-        gra_s[pl.ds(i * per, per)] = block.reshape(per, SLOTS, width)
-
-    both_ways(8, gra_s, gra_a, gra_b, gra_r)
-
     grad1 = tn(zprod, d_pre)
     gb1 = jnp.sum(d_pre.astype(F32), axis=0, keepdims=True)
     gd2 = jnp.sum(hidden * dlogit, axis=0, keepdims=True)
@@ -338,25 +337,40 @@
         pltpu.make_async_copy(source(z), goal(z), rsem.at[index]).start()
         sent.append((index, sent_size))
 
+    dz = nt(d_pre, wdec1[...])
+    gpair[:queries, :] = (dz * tail).astype(BF)
+    gpair[queries:, :] = (dz * head).astype(BF)
+
+    @pl.loop(0, slots // gtile)
+    def _(i):
+        at = pl.ds(pl.multiple_of(i * gtile, gtile), gtile)
+        block = nn(hot_et[at, :], gpair[...]).astype(BF)
+        gra_s[pl.ds(i * per, per)] = block.reshape(per, SLOTS, width)
+
+    gra_s4 = gra_s.reshape(n_y, n_zc, SLOTS, width)
+    along_y(9, lambda p: gra_s4.at[p, :, :, right], lambda m: gra_b.at[m], gra_b.at[pl.ds(0, n_y - 1)])
+
     pair.wait_recv()
     for j in range(n_z):
-        dz_s[j, :zrows] = dc_s[core, j * zrows : (j + 1) * zrows] + dc_r[j * zrows : (j + 1) * zrows]
-        dz_s[j, zrows:] = dc_s[core, crows:] + dc_r[crows:]
+        dz_s[j, :zrows] = (dc_s[core, j * zrows : (j + 1) * zrows] + dc_r[j * zrows : (j + 1) * zrows]).astype(BF)
+        dz_s[j, zrows:] = (dc_s[core, crows:] + dc_r[crows:]).astype(BF)
     along_z(13, lambda p: dz_s.at[p], lambda m: dz_r.at[m], dz_s.at[pl.ds(0, n_z - 1)])
 
+    along_zc(8, lambda p: gra_s4.at[:, p, :, left], lambda m: gra_a.at[m], gra_a.at[pl.ds(0, n_zc - 1)])
+
+    copies(dz_r, rsem.at[13]).wait()
+    total = dz_r[0].astype(F32)
+    for j in range(1, n_z):
+        total = total + dz_r[j].astype(F32)
+    zbuf[...] = total.astype(BF)
+    along_y(14, lambda p: zbuf, lambda m: dy_r.at[m], dy_r.at[pl.ds(0, n_y - 1)])
+
     both_ways_on(8, gra_a, gra_b, gra_r)
 
-    copies(dz_r, rsem.at[13]).wait()
-    total = dz_r[0]
-    for j in range(1, n_z):
-        total = total + dz_r[j]
-    zbuf[...] = total
-    along_y(14, lambda p: zbuf, lambda m: dy_r.at[m], dy_r.at[pl.ds(0, n_y - 1)])
-
     copies(dy_r, rsem.at[14]).wait()
-    total = dy_r[0]
+    total = dy_r[0].astype(F32)
     for j in range(1, n_y):
-        total = total + dy_r[j]
+        total = total + dy_r[j].astype(F32)
     dbuf[...] = total
     for k in range(1, n_x):
         pltpu.make_async_remote_copy(
@@ -366,15 +380,23 @@
     pltpu.make_async_copy(dbuf, dx_r.at[rep], rsem.at[15]).start()
     sent.append((15, dx_r.at[pl.ds(0, n_x - 1)]))
 
+    copies(dx_r, rsem.at[15]).wait()
+    total = dx_r[0]
+    for j in range(1, n_x):
+        total = total + dx_r[j]
+    gv_o[...] = total[zrows:]
+    dc_r[:zrows] = total[:zrows]
+    along_z(20, lambda p: dc_r.at[pl.ds(0, zrows)], lambda m: dg_r.at[core, m], dg_r.at[0, pl.ds(0, n_z - 1)])
+
     flip = rep + 1 - 2 * lax.rem(rep, 2)
     wrap = 3 - rep
     wflip = wrap + 1 - 2 * lax.rem(wrap, 2)
     quarter = nodes // n_x
     jtile = min(64, quarter)
 
-    def local_sum(q, cols):
+    def local_sum(q):
         at = pl.ds(pl.multiple_of(q * quarter, quarter), quarter)
-        return nn(hot_gt[at, :], gra_r[cols].reshape(slots, half))
+        return nn(hot_gt[at, :], gra_r[...].reshape(slots, width))
 
     def trade(index, source, goal, partner):
         copy = pltpu.make_async_remote_copy(
@@ -390,33 +412,28 @@
             at = pl.ds(pl.multiple_of(i * jtile, jtile), jtile)
             xs2[way, at, :] = (xk[part, at, :] + xr1[way, 1, at, :].astype(F32)).astype(BF)
 
-    copies(gra_r.at[0], rsem.at[10]).wait()
-    xs1[0, 0] = local_sum(flip, 0).astype(BF)
-    xs1[0, 1] = local_sum(wflip, 0).astype(BF)
+    copies(gra_r.at[:, :, :, left], rsem.at[10]).wait()
+    copies(gra_r.at[:, :, :, right], rsem.at[11]).wait()
+    part = local_sum(wflip)
+    xs1[0, 1] = part[:, :half].astype(BF)
+    xs1[1, 1] = part[:, half:].astype(BF)
+    part = local_sum(flip)
+    xs1[0, 0] = part[:, :half].astype(BF)
     one = trade(16, xs1.at[0], xr1.at[0], flip)
-    copies(gra_r.at[1], rsem.at[11]).wait()
-    xs1[1, 0] = local_sum(wrap, 1).astype(BF)
-    xs1[1, 1] = local_sum(wflip, 1).astype(BF)
+    xk[3] = part[:, half:]
+    part = local_sum(wrap)
+    xs1[1, 0] = part[:, half:].astype(BF)
     two = trade(17, xs1.at[1], xr1.at[1], wrap)
-    xk[0] = local_sum(rep, 0)
-    xk[1] = local_sum(rep, 1)
-    xk[2] = local_sum(wrap, 0)
-    xk[3] = local_sum(flip, 1)
+    xk[2] = part[:, :half]
+    part = local_sum(rep)
+    xk[0] = part[:, :half]
+    xk[1] = part[:, half:]
     one.wait_recv()
     joined(0, 2)
     three = trade(18, xs2.at[0], xr2.at[0], wrap)
     two.wait_recv()
     joined(1, 3)
     four = trade(19, xs2.at[1], xr2.at[1], flip)
-
-    copies(dx_r, rsem.at[15]).wait()
-    total = dx_r[0]
-    for j in range(1, n_x):
-        total = total + dx_r[j]
-    zbuf2 = total[:zrows]
-    gv_o[...] = total[zrows:]
-    dc_r[:zrows] = zbuf2
-    along_z(20, lambda p: dc_r.at[pl.ds(0, zrows)], lambda m: dg_r.at[core, m], dg_r.at[0, pl.ds(0, n_z - 1)])
 
     three.wait_recv()
     ge_o[:, :half] = xk[0] + xr1[0, 0].astype(F32) + xr2[0].astype(F32)
@@ -481,22 +498,23 @@
             V((nodes, width), BF), V((nodes, width), BF), V((nodes, nodes), BF), V((nodes, halos), BF),
             V((width, width), BF), V((width, width), BF), V((width, width), BF),
             V((n_zc, n_y, LANES), BF), V((n_zc, n_y, LANES), BF), V((n_y, n_zc, LANES), BF), V((n_y, n_zc, LANES), BF),
-            V((n_zc, 2, n_y, width), BF), V((n_zc, 2, n_y, width), BF), V((n_y, 2 * n_zc, width), BF),
-            V((n_y, 2 * n_zc, width), BF), V((nodes, halos), BF),
+            V((n_zc, 2, n_y, half), BF), V((n_zc, 2, n_y, half), BF), V((n_y, 2 * n_zc, half), BF),
+            V((n_y, 2 * n_zc, half), BF), V((n_zc, 2, n_y, half), BF), V((n_y, 2 * n_zc, half), BF),
+            V((n_y, 2 * n_zc, half), BF), V((n_zc, 2, n_y, half), BF), V((halos, width), BF), V((nodes, halos), BF),
             V((nodes, width), F32), V((nodes, width), F32), V((8, ends), F32),
             V((ends, slots), BF), V((slots, ends), BF), V((slots, nodes), BF), V((nodes, slots), BF),
             V((n_dom, SLOTS, width), BF), V((n_zc, n_y, SLOTS, half), BF), V((n_y, n_zc, SLOTS, half), BF),
-            V((2, n_y, n_zc, SLOTS, half), BF),
+            V((n_y, n_zc, SLOTS, width), BF),
             V((n_dom, SLOTS, width), BF), V((n_zc, n_y, SLOTS, half), BF), V((n_y, n_zc, SLOTS, half), BF),
-            V((2, n_y, n_zc, SLOTS, half), BF), V((ends, width), BF),
-            V((zrows + 8, width), F32), V((zrows + 8, width), F32),
+            V((n_y, n_zc, SLOTS, width), BF), V((ends, width), BF),
+            V((zrows + 8, width), BF), V((zrows + 8, width), F32),
             V((2, 2, quarter, half), BF), V((2, 2, quarter, half), BF), V((2, quarter, half), BF),
             V((2, quarter, half), BF), V((4, quarter, half), F32),
             V((2, crows + 8, width), F32), V((crows + 8, width), F32),
-            V((n_z, zrows + 8, width), F32), V((n_z, zrows + 8, width), F32),
-            V((n_y, zrows + 8, width), F32), V((n_x, zrows + 8, width), F32), V((2, n_z, zrows, width), F32),
+            V((n_z, zrows + 8, width), BF), V((n_z, zrows + 8, width), BF),
+            V((n_y, zrows + 8, width), BF), V((n_x, zrows + 8, width), F32), V((2, n_z, zrows, width), F32),
             pltpu.SemaphoreType.DMA((7,)), pltpu.SemaphoreType.DMA((4,)),
-            pltpu.SemaphoreType.DMA((22,)), pltpu.SemaphoreType.DMA((22,)),
+            pltpu.SemaphoreType.DMA((24,)), pltpu.SemaphoreType.DMA((24,)),
         ],
         compiler_params=pltpu.CompilerParams(
             collective_id=0, has_side_effects=True, vmem_limit_bytes=60 * 1024 * 1024

time: 98.5 us -> 92.9 us (0.943)
  Pallas kernels: 97.7 us -> 92.2 us
    pallas_call x1, Pallas kernels: 96.7 us -> 91.1 us  [per_device(): pl.pallas_call(functools.partial(kernel, n_y, n_zc, n_x), out_shape=(V((n...]
where the time goes in v3:
time: 92.9 us; the launch traced here: 92.8 us
  Pallas kernels  92.2 us (99%)
    pallas_call x1, Pallas kernels, per_device(): pl.pallas_call(functools.partial(kernel, n_y, n_zc, n_x), out_shape=(V((n...  91.1 us

profile of v3, /device:TPU:1, one launch (start us, length us, event | category | flops | bytes accessed | tf_op | source)
XLA Modules:
  0.0 92.8 jit_solution(13756338149485389878)
XLA Ops:
  0.6 91.1 %encode_decode.1 = (bf16[1024,256]{1,0:T(8,128)(2,1)S(1)}, f32[256,256]{1,0:T(8,128)S(1)}, f32[256,256]{1,0:T(8,128)S(1)}, f32[8,256]{1,0:T(8,128)S(1)}) custom-call(s32[2,256]{1,0:T(2,128)} %bitcast.8, s32[2,256]{1,0:T(2,128)} %bitcast.9, s32[2,128]{1,0:T(2,128)} %bitcast.10, s32[1,256]{1,0:T(1,128)} %bitcast.11, f32[1,256]{1,0:T(1,128)} %bitcast.12, ...), custom_call_target="tpu_custom_call" | custom-call | tf_op jit(solution)/shard_map/encode_decode/pallas_call | solution.py:487
  91.8 1.0 %put_out.1 = (bf16[1024,256]{1,0:T(8,128)(2,1)}, f32[256,256]{1,0:T(8,128)}, f32[256,256]{1,0:T(8,128)}, f32[1,256]{1,0:T(1,128)}, f32[1,256]{1,0:T(1,128)}) custom-call(bf16[1024,256]{1,0:T(8,128)(2,1)S(1)} %get-tuple-element.14.emb, f32[256,256]{1,0:T(8,128)S(1)} %get-tuple-element.15.ge, f32[256,256]{1,0:T(8,128)S(1)} %get-tuple-element.16.gd, ...), custom_call_target="tpu_custom_call" | custom-call | tf_op jit(solution)/shard_map/put_out/pallas_call | solution.py:528

commit v4 on v3

--- a/solution.py
+++ b/solution.py
@@ -49,15 +49,20 @@
     return jnp.sum(jnp.where(iota((n, n), 0) == iota((n, n), 1), column, 0.0), axis=0, keepdims=True)
 
 
+def far_first(n):
+    return sorted(range(1, n), key=lambda k: -min(k, n - k))
+
+
 def copies(ref, sem):
     return pltpu.make_async_copy(ref, ref, sem)
 
 
 def kernel(
     n_y, n_zc, n_x,
-    eo, er, hr, lab, b_enc, b_dec1, w_dec2,
+    eo_h, er_h, hr_h, lab_h, b_enc_h, b_dec1_h, w_dec2_h,
     feats_h, hist_h, adji_h, adjh_h, wself_h, wnbr_h, wdec1_h,
     emb_o, ge_o, gd_o, gv_o,
+    eo, er, hr, lab, b_enc, b_dec1, w_dec2,
     feats, hist, adji, adjh, wself, wnbr, wdec1,
     ids_s, ids_r1, ids_t, ids_r2,
     hal_s, hal_r1, hal_t, hal_r2, hal_m, hal_u, hal_v, hal_w, halo, adjp,
@@ -68,7 +73,7 @@
     zbuf, dbuf,
     xs1, xr1, xs2, xr2, xk,
     dc_s, dc_r, dz_s, dz_r, dy_r, dx_r, dg_r,
-    load_sem, out_sem,
+    small_sem, load_sem,
     ssem, rsem,
 ):
     n_dom = n_y * n_zc
@@ -87,15 +92,18 @@
     z = lax.div(zc, 2)
     core = lax.rem(zc, 2)
 
+    small = [
+        pltpu.make_async_copy(src, dst, small_sem.at[i])
+        for i, (src, dst) in enumerate(
+            ((eo_h, eo), (er_h, er), (hr_h, hr), (lab_h, lab), (b_enc_h, b_enc), (b_dec1_h, b_dec1), (w_dec2_h, w_dec2))
+        )
+    ]
     loads = [
         pltpu.make_async_copy(src, dst, load_sem.at[i])
         for i, (src, dst) in enumerate(
             ((feats_h, feats), (adji_h, adji), (wself_h, wself), (adjh_h, adjh), (hist_h, hist), (wnbr_h, wnbr), (wdec1_h, wdec1))
         )
     ]
-    for load in loads:
-        load.start()
-
     barrier = pltpu.get_barrier_semaphore()
 
     def zc_peer(k):
@@ -104,16 +112,10 @@
     def y_peer(k):
         return lax.rem(y + k, n_y)
 
-    def greet_zc(k, carry):
+    for k in far_first(n_zc):
         pl.semaphore_signal(barrier, inc=1, device_id={"dom": y * n_zc + zc_peer(k)}, device_id_type=MESH)
-        return carry
-
-    def greet_y(k, carry):
+    for k in far_first(n_y):
         pl.semaphore_signal(barrier, inc=1, device_id={"dom": y_peer(k) * n_zc + zc}, device_id_type=MESH)
-        return carry
-
-    lax.fori_loop(1, n_zc, greet_zc, 0)
-    lax.fori_loop(1, n_y, greet_y, 0)
     for k in range(1, n_x):
         pl.semaphore_signal(barrier, inc=1, device_id={"rep": lax.rem(rep + k, n_x)}, device_id_type=MESH)
 
@@ -124,30 +126,29 @@
             copies(size, ssem.at[index]).wait()
 
     def along_zc(index, source, target, sent_size):
-        def body(k, carry):
+        for k in far_first(n_zc):
             peer = zc_peer(k)
             pltpu.make_async_remote_copy(
                 src_ref=source(peer), dst_ref=target(zc), send_sem=ssem.at[index], recv_sem=rsem.at[index],
                 device_id={"dom": y * n_zc + peer}, device_id_type=MESH,
             ).start()
-            return carry
-
-        lax.fori_loop(1, n_zc, body, 0)
         pltpu.make_async_copy(source(zc), target(zc), rsem.at[index]).start()
         sent.append((index, sent_size))
 
     def along_y(index, source, target, sent_size):
-        def body(k, carry):
+        for k in far_first(n_y):
             peer = y_peer(k)
             pltpu.make_async_remote_copy(
                 src_ref=source(peer), dst_ref=target(y), send_sem=ssem.at[index], recv_sem=rsem.at[index],
                 device_id={"dom": peer * n_zc + zc}, device_id_type=MESH,
             ).start()
-            return carry
-
-        lax.fori_loop(1, n_y, body, 0)
         pltpu.make_async_copy(source(y), target(y), rsem.at[index]).start()
         sent.append((index, sent_size))
+
+    for load in small + loads:
+        load.start()
+    for load in small:
+        load.wait()
 
     owner = jnp.concatenate([eo[0:1, :], eo[1:2, :]], axis=1)
     local = jnp.concatenate([er[0:1, :], er[1:2, :]], axis=1)
@@ -206,22 +207,14 @@
     for i in (4, 5, 6):
         loads[i].wait()
 
-    place_col = column_of(place[0:1, :])
-    etile = min(256, ends)
-    for i in range(ends // etile):
-        hot_e[i * etile : (i + 1) * etile, :] = hot(
-            place_col[i * etile : (i + 1) * etile, :] == iota((etile, slots), 1).astype(F32)
-        )
-
     copies(ids_r2, rsem.at[1]).wait()
     asked = nn(to_zc_y, ids_r2[...].reshape(n_dom, LANES))
+    asked_c = [32.0 * asked[:, at : at + 1] + asked[:, at + 16 : at + 17] for at in (SLOTS, SLOTS + 1)]
+    pick = hot(jnp.concatenate(asked_c, axis=0) == iota((halos, nodes), 1).astype(F32))
+    picked = nn(pick, hist[...]).astype(BF)
     for c in range(2):
-        at = SLOTS + c
-        asked_c = 32.0 * asked[:, at : at + 1] + asked[:, at + 16 : at + 17]
-        pick = hot(asked_c == iota((n_dom, nodes), 1).astype(F32))
-        picked = nn(pick, hist[...]).astype(BF)
-        hal_s[:, c] = picked[:, :half].reshape(n_zc, n_y, half)
-        hal_m[:, c] = picked[:, half:].reshape(n_zc, n_y, half)
+        hal_s[:, c] = picked[c * n_dom : (c + 1) * n_dom, :half].reshape(n_zc, n_y, half)
+        hal_m[:, c] = picked[c * n_dom : (c + 1) * n_dom, half:].reshape(n_zc, n_y, half)
     along_zc(2, lambda p: hal_s.at[p], lambda m: hal_r1.at[m], hal_s.at[pl.ds(0, n_zc - 1)])
     io, oo = iota((halos, halos), 1), iota((halos, halos), 0)
     turn = hot(io == ((oo & (n_zc - 1)) << (ly + 1)) + (((oo >> lzc) & 1) << ly) + (oo >> (lzc + 1)))
@@ -249,18 +242,6 @@
     hal_m[...] = nn(back, hal_v[...].reshape(halos, half)).astype(BF).reshape(n_zc, 2, n_y, half)
     along_zc(23, lambda p: hal_m.at[p], lambda m: hal_w.at[m], hal_m.at[pl.ds(0, n_zc - 1)])
 
-    @pl.loop(0, nodes // tile)
-    def _(i):
-        at = pl.ds(pl.multiple_of(i * tile, tile), tile)
-        hot_gt[at, :] = hot((iota((tile, slots), 0) + i * tile).astype(F32) == id_row)
-
-    @pl.loop(0, slots // gtile)
-    def _(i):
-        at = pl.ds(pl.multiple_of(i * gtile, gtile), gtile)
-        hot_et[at, :] = hot((iota((gtile, ends), 0) + i * gtile).astype(F32) == place[0:1, :])
-
-    target = column_of(lab[...].astype(F32))
-
     copies(hal_r2, rsem.at[3]).wait()
     copies(hal_w, rsem.at[23]).wait()
     halo[:, :half] = hal_r2[...].reshape(halos, half)
@@ -292,7 +273,27 @@
         along_zc(base + 3, lambda p: mid_b.at[:, p], lambda m: recv.at[:, m, :, right], mid_a.at[pl.ds(0, n_zc - 1)])
 
     both_ways(4, fet_s, fet_a, fet_b, fet_r)
+    place_col = column_of(place[0:1, :])
+    etile = min(256, ends)
+    for i in range(ends // etile):
+        hot_e[i * etile : (i + 1) * etile, :] = hot(
+            place_col[i * etile : (i + 1) * etile, :] == iota((etile, slots), 1).astype(F32)
+        )
+
+    @pl.loop(0, slots // gtile)
+    def _(i):
+        at = pl.ds(pl.multiple_of(i * gtile, gtile), gtile)
+        hot_et[at, :] = hot((iota((gtile, ends), 0) + i * gtile).astype(F32) == place[0:1, :])
+
+    target = column_of(lab[...].astype(F32))
+
     both_ways_on(4, fet_a, fet_b, fet_r)
+
+    @pl.loop(0, nodes // tile)
+    def _(i):
+        at = pl.ds(pl.multiple_of(i * tile, tile), tile)
+        hot_gt[at, :] = hot((iota((tile, slots), 0) + i * tile).astype(F32) == id_row)
+
     copies(fet_r.at[:, :, :, left], rsem.at[6]).wait()
     copies(fet_r.at[:, :, :, right], rsem.at[7]).wait()
 
@@ -325,15 +326,12 @@
     pair.start()
 
     def along_z(index, source, goal, sent_size):
-        def body(k, carry):
+        for k in far_first(n_z):
             peer = lax.rem(z + k, n_z)
             pltpu.make_async_remote_copy(
                 src_ref=source(peer), dst_ref=goal(z), send_sem=ssem.at[index], recv_sem=rsem.at[index],
                 device_id={"dom": y * n_zc + 2 * peer + core}, device_id_type=MESH,
             ).start()
-            return carry
-
-        lax.fori_loop(1, n_z, body, 0)
         pltpu.make_async_copy(source(z), goal(z), rsem.at[index]).start()
         sent.append((index, sent_size))
 
@@ -435,17 +433,17 @@
     joined(1, 3)
     four = trade(19, xs2.at[1], xr2.at[1], flip)
 
-    three.wait_recv()
-    ge_o[:, :half] = xk[0] + xr1[0, 0].astype(F32) + xr2[0].astype(F32)
-    four.wait_recv()
-    ge_o[:, half:] = xk[1] + xr1[1, 0].astype(F32) + xr2[1].astype(F32)
-
     copies(dg_r.at[0], rsem.at[20]).wait()
     last = pltpu.make_async_remote_copy(
         src_ref=dg_r.at[core], dst_ref=dg_r.at[core], send_sem=ssem.at[21], recv_sem=rsem.at[21],
         device_id={"dom": y * n_zc + 2 * z + other}, device_id_type=MESH,
     )
     last.start()
+
+    three.wait_recv()
+    ge_o[:, :half] = xk[0] + xr1[0, 0].astype(F32) + xr2[0].astype(F32)
+    four.wait_recv()
+    ge_o[:, half:] = xk[1] + xr1[1, 0].astype(F32) + xr2[1].astype(F32)
 
     drain()
     pair.wait_send()
@@ -492,9 +490,11 @@
             V((width, width), F32),
             V((8, width), F32),
         ),
-        in_specs=[vmem] * 7 + [any_] * 7,
+        in_specs=[any_] * 14,
         out_specs=(vmem,) * 4,
         scratch_shapes=[
+            V((2, queries), I32), V((2, queries), I32), V((2, n_dom), I32), V((1, queries), I32), V((1, width), F32),
+            V((1, width), F32), V((width,), BF),
             V((nodes, width), BF), V((nodes, width), BF), V((nodes, nodes), BF), V((nodes, halos), BF),
             V((width, width), BF), V((width, width), BF), V((width, width), BF),
             V((n_zc, n_y, LANES), BF), V((n_zc, n_y, LANES), BF), V((n_y, n_zc, LANES), BF), V((n_y, n_zc, LANES), BF),
@@ -513,7 +513,7 @@
             V((2, crows + 8, width), F32), V((crows + 8, width), F32),
             V((n_z, zrows + 8, width), BF), V((n_z, zrows + 8, width), BF),
             V((n_y, zrows + 8, width), BF), V((n_x, zrows + 8, width), F32), V((2, n_z, zrows, width), F32),
-            pltpu.SemaphoreType.DMA((7,)), pltpu.SemaphoreType.DMA((4,)),
+            pltpu.SemaphoreType.DMA((7,)), pltpu.SemaphoreType.DMA((7,)),
             pltpu.SemaphoreType.DMA((24,)), pltpu.SemaphoreType.DMA((24,)),
         ],
         compiler_params=pltpu.CompilerParams(

time: 92.9 us -> 85.5 us (0.920)
  Pallas kernels: 92.2 us -> 84.2 us
    pallas_call x1, Pallas kernels: 91.1 us -> 83.2 us  [per_device(): pl.pallas_call(functools.partial(kernel, n_y, n_zc, n_x), out_shape=(V((n...]
where the time goes in v4:
time: 85.5 us; the launch traced here: 84.9 us
  Pallas kernels  84.2 us (98%)
    pallas_call x1, Pallas kernels, per_device(): pl.pallas_call(functools.partial(kernel, n_y, n_zc, n_x), out_shape=(V((n...  83.2 us

profile of v4, /device:TPU:1, one launch (start us, length us, event | category | flops | bytes accessed | tf_op | source)
XLA Modules:
  0.0 84.9 jit_solution(15719979893781672267)
XLA Ops:
  0.6 83.2 %encode_decode.1 = (bf16[1024,256]{1,0:T(8,128)(2,1)S(1)}, f32[256,256]{1,0:T(8,128)S(1)}, f32[256,256]{1,0:T(8,128)S(1)}, f32[8,256]{1,0:T(8,128)S(1)}) custom-call(s32[2,256]{1,0:T(2,128)} %bitcast.8, s32[2,256]{1,0:T(2,128)} %bitcast.9, s32[2,128]{1,0:T(2,128)} %bitcast.10, s32[1,256]{1,0:T(1,128)} %bitcast.11, f32[1,256]{1,0:T(1,128)} %bitcast.12, ...), custom_call_target="tpu_custom_call" | custom-call | tf_op jit(solution)/shard_map/encode_decode/pallas_call | solution.py:485
  83.9 1.0 %put_out.1 = (bf16[1024,256]{1,0:T(8,128)(2,1)}, f32[256,256]{1,0:T(8,128)}, f32[256,256]{1,0:T(8,128)}, f32[1,256]{1,0:T(1,128)}, f32[1,256]{1,0:T(1,128)}) custom-call(bf16[1024,256]{1,0:T(8,128)(2,1)S(1)} %get-tuple-element.14.emb, f32[256,256]{1,0:T(8,128)S(1)} %get-tuple-element.15.ge, f32[256,256]{1,0:T(8,128)S(1)} %get-tuple-element.16.gd, ...), custom_call_target="tpu_custom_call" | custom-call | tf_op jit(solution)/shard_map/put_out/pallas_call | solution.py:528

commit v5 on v4

--- a/solution.py
+++ b/solution.py
@@ -51,6 +51,19 @@
 
 def far_first(n):
     return sorted(range(1, n), key=lambda k: -min(k, n - k))
+
+
+def offset_at(place, n):
+    return jnp.where((place & 1) == 1, n // 2 - ((place + 1) >> 1), n // 2 + (place >> 1))
+
+
+def place_of(offset, n):
+    d = (offset & (n - 1)) - n // 2
+    return jnp.where(d < 0, -2 * d - 1, 2 * d)
+
+
+def far_places(n):
+    return [n // 2 - (p + 1) // 2 if p % 2 else n // 2 + p // 2 for p in range(n)]
 
 
 def copies(ref, sem):
@@ -66,7 +79,7 @@
     feats, hist, adji, adjh, wself, wnbr, wdec1,
     ids_s, ids_r1, ids_t, ids_r2,
     hal_s, hal_r1, hal_t, hal_r2, hal_m, hal_u, hal_v, hal_w, halo, adjp,
-    inner, selfp, place,
+    inner, selfp, place, far_place,
     hot_e, hot_et, hot_g, hot_gt,
     fet_s, fet_a, fet_b, fet_r,
     gra_s, gra_a, gra_b, gra_r, gpair,
@@ -160,6 +173,8 @@
     rank = nn(match_hot, before)
     slot = jnp.sum(jnp.where(match, rank, 0.0), axis=0, keepdims=True)
     place[...] = jnp.broadcast_to(owner.astype(F32) * float(SLOTS) + slot, place.shape)
+    far = (place_of((owner >> lzc) - y, n_y) << lzc) + place_of((owner & (n_zc - 1)) - zc, n_zc)
+    far_place[...] = jnp.broadcast_to(far.astype(F32) * float(SLOTS) + slot, far_place.shape)
 
     def lane_rows(at, value):
         lane = iota((LANES, value.shape[1]), 0)
@@ -224,16 +239,20 @@
 
     gtile = min(256, slots)
     per = gtile // SLOTS
-    id_rows = []
+
+    def ids_column(asked):
+        n = asked.shape[0] * SLOTS
+        spread = jnp.broadcast_to(asked[:, None, :], (asked.shape[0], SLOTS, LANES)).reshape(n, LANES)
+        lane, mine = iota((n, LANES), 1), iota((n, LANES), 0) & (SLOTS - 1)
+        weight = jnp.where(lane == mine, 32.0, jnp.where(lane == mine + 16, 1.0, 0.0))
+        return jnp.sum(spread * weight, axis=1, keepdims=True)
+
+    by_y = (offset_at(prow >> lzc, n_y) + y) & (n_y - 1)
+    by_zc = (offset_at(prow & (n_zc - 1), n_zc) + zc) & (n_zc - 1)
+    asked_far = nn(hot(pcol == (by_y << lzc) + by_zc), ids_r2[...].reshape(n_dom, LANES))
     for i in range(slots // gtile):
-        asked = ids_r2[...].reshape(n_dom, LANES)[i * per : (i + 1) * per].astype(F32)
-        spread = jnp.broadcast_to(asked[:, None, :], (per, SLOTS, LANES)).reshape(gtile, LANES)
-        lane, mine = iota((gtile, LANES), 1), iota((gtile, LANES), 0) & (SLOTS - 1)
-        weight = jnp.where(lane == mine, 32.0, jnp.where(lane == mine + 16, 1.0, 0.0))
-        id_col = jnp.sum(spread * weight, axis=1, keepdims=True)
+        id_col = ids_column(asked_far[i * per : (i + 1) * per])
         hot_g[i * gtile : (i + 1) * gtile, :] = hot(id_col == iota((gtile, nodes), 1).astype(F32))
-        id_rows.append(row_of(id_col))
-    id_row = jnp.concatenate(id_rows, axis=1)
 
     copies(hal_r1, rsem.at[2]).wait()
     hal_t[...] = nn(turn, hal_r1[...].reshape(halos, half)).astype(BF).reshape(n_y, 2 * n_zc, half)
@@ -261,18 +280,74 @@
 
     left, right = pl.ds(0, half), pl.ds(half, half)
 
-    def both_ways(base, send, mid_a, mid_b, recv):
-        send4 = send.reshape(n_y, n_zc, SLOTS, width)
-        along_zc(base, lambda p: send4.at[:, p, :, left], lambda m: mid_a.at[m], mid_a.at[pl.ds(0, n_zc - 1)])
-        along_y(base + 1, lambda p: send4.at[p, :, :, right], lambda m: mid_b.at[m], mid_b.at[pl.ds(0, n_y - 1)])
-
-    def both_ways_on(base, mid_a, mid_b, recv):
-        copies(mid_a, rsem.at[base]).wait()
-        along_y(base + 2, lambda p: mid_a.at[:, p], lambda m: recv.at[m, :, :, left], mid_b.at[pl.ds(0, n_y - 1)])
-        copies(mid_b, rsem.at[base + 1]).wait()
-        along_zc(base + 3, lambda p: mid_b.at[:, p], lambda m: recv.at[:, m, :, right], mid_a.at[pl.ds(0, n_zc - 1)])
-
-    both_ways(4, fet_s, fet_a, fet_b, fet_r)
+    y_off, zc_off = far_places(n_y), far_places(n_zc)
+    y_part, zc_part = n_y // 2, n_zc // 2
+
+    def send_to(index, peer, source, goal, signal):
+        pltpu.make_async_remote_copy(
+            src_ref=source, dst_ref=goal, send_sem=ssem.at[index], recv_sem=rsem.at[signal],
+            device_id={"dom": peer}, device_id_type=MESH,
+        ).start()
+
+    def zc_at(p):
+        return lax.rem(zc + zc_off[p], n_zc)
+
+    def y_at(p):
+        return lax.rem(y + y_off[p], n_y)
+
+    def first_hop_zc(base, send, mid, group):
+        ys = pl.ds(group * y_part, y_part)
+        for p in range(n_zc):
+            source, goal = send.at[ys, p, :, left], mid.at[zc, ys]
+            if zc_off[p]:
+                send_to(base, y * n_zc + zc_at(p), source, goal, base + 2 * group)
+            else:
+                pltpu.make_async_copy(source, goal, rsem.at[base + 2 * group]).start()
+
+    def first_hop_y(base, send, mid, group):
+        zcs = pl.ds(group * zc_part, zc_part)
+        for p in range(n_y):
+            source, goal = send.at[p, zcs, :, right], mid.at[y, zcs]
+            if y_off[p]:
+                send_to(base + 1, y_at(p) * n_zc + zc, source, goal, base + 1 + 2 * group)
+            else:
+                pltpu.make_async_copy(source, goal, rsem.at[base + 1 + 2 * group]).start()
+
+    def second_hop_y(base, mid, recv, group):
+        copies(mid.at[:, pl.ds(group * y_part, y_part)], rsem.at[base + 2 * group]).wait()
+        for p in range(group * y_part, (group + 1) * y_part):
+            source, goal = mid.at[:, p], recv.at[y, :, :, left]
+            if y_off[p]:
+                send_to(base + 2, y_at(p) * n_zc + zc, source, goal, base + 4)
+            else:
+                pltpu.make_async_copy(source, goal, rsem.at[base + 4]).start()
+
+    def second_hop_zc(base, mid, recv, group):
+        copies(mid.at[:, pl.ds(group * zc_part, zc_part)], rsem.at[base + 1 + 2 * group]).wait()
+        for p in range(group * zc_part, (group + 1) * zc_part):
+            source, goal = mid.at[:, p], recv.at[:, zc, :, right]
+            if zc_off[p]:
+                send_to(base + 3, y * n_zc + zc_at(p), source, goal, base + 5)
+            else:
+                pltpu.make_async_copy(source, goal, rsem.at[base + 5]).start()
+
+    def second_hops(base, mid_a, mid_b, recv):
+        for group in range(2):
+            second_hop_y(base, mid_a, recv, group)
+            second_hop_zc(base, mid_b, recv, group)
+        sent.append((base, mid_a.at[pl.ds(0, n_zc - 1)]))
+        sent.append((base + 1, mid_b.at[pl.ds(0, n_y - 1)]))
+        sent.append((base + 2, mid_b.at[pl.ds(0, n_y - 1)]))
+        sent.append((base + 3, mid_a.at[pl.ds(0, n_zc - 1)]))
+
+    def arrived(base, recv):
+        copies(recv.at[:, :, :, left], rsem.at[base + 4]).wait()
+        copies(recv.at[:, :, :, right], rsem.at[base + 5]).wait()
+
+    fet_s4, gra_s4 = (send.reshape(n_y, n_zc, SLOTS, width) for send in (fet_s, gra_s))
+    for group in range(2):
+        first_hop_zc(24, fet_s4, fet_a, group)
+        first_hop_y(24, fet_s4, fet_b, group)
     place_col = column_of(place[0:1, :])
     etile = min(256, ends)
     for i in range(ends // etile):
@@ -283,19 +358,23 @@
     @pl.loop(0, slots // gtile)
     def _(i):
         at = pl.ds(pl.multiple_of(i * gtile, gtile), gtile)
-        hot_et[at, :] = hot((iota((gtile, ends), 0) + i * gtile).astype(F32) == place[0:1, :])
+        hot_et[at, :] = hot((iota((gtile, ends), 0) + i * gtile).astype(F32) == far_place[0:1, :])
 
     target = column_of(lab[...].astype(F32))
 
-    both_ways_on(4, fet_a, fet_b, fet_r)
+    second_hops(24, fet_a, fet_b, fet_r)
+
+    asked = ids_r2[...].reshape(n_dom, LANES).astype(F32)
+    id_row = jnp.concatenate(
+        [row_of(ids_column(asked[i * per : (i + 1) * per])) for i in range(slots // gtile)], axis=1
+    )
 
     @pl.loop(0, nodes // tile)
     def _(i):
         at = pl.ds(pl.multiple_of(i * tile, tile), tile)
         hot_gt[at, :] = hot((iota((tile, slots), 0) + i * tile).astype(F32) == id_row)
 
-    copies(fet_r.at[:, :, :, left], rsem.at[6]).wait()
-    copies(fet_r.at[:, :, :, right], rsem.at[7]).wait()
+    arrived(24, fet_r)
 
     got = fet_r[...].reshape(slots, width)
     head = nn(hot_e[:queries, :], got)
@@ -345,8 +424,8 @@
         block = nn(hot_et[at, :], gpair[...]).astype(BF)
         gra_s[pl.ds(i * per, per)] = block.reshape(per, SLOTS, width)
 
-    gra_s4 = gra_s.reshape(n_y, n_zc, SLOTS, width)
-    along_y(9, lambda p: gra_s4.at[p, :, :, right], lambda m: gra_b.at[m], gra_b.at[pl.ds(0, n_y - 1)])
+    for group in range(2):
+        first_hop_y(30, gra_s4, gra_b, group)
 
     pair.wait_recv()
     for j in range(n_z):
@@ -354,7 +433,8 @@
         dz_s[j, zrows:] = (dc_s[core, crows:] + dc_r[crows:]).astype(BF)
     along_z(13, lambda p: dz_s.at[p], lambda m: dz_r.at[m], dz_s.at[pl.ds(0, n_z - 1)])
 
-    along_zc(8, lambda p: gra_s4.at[:, p, :, left], lambda m: gra_a.at[m], gra_a.at[pl.ds(0, n_zc - 1)])
+    for group in range(2):
+        first_hop_zc(30, gra_s4, gra_a, group)
 
     copies(dz_r, rsem.at[13]).wait()
     total = dz_r[0].astype(F32)
@@ -363,7 +443,7 @@
     zbuf[...] = total.astype(BF)
     along_y(14, lambda p: zbuf, lambda m: dy_r.at[m], dy_r.at[pl.ds(0, n_y - 1)])
 
-    both_ways_on(8, gra_a, gra_b, gra_r)
+    second_hops(30, gra_a, gra_b, gra_r)
 
     copies(dy_r, rsem.at[14]).wait()
     total = dy_r[0].astype(F32)
@@ -410,8 +490,7 @@
             at = pl.ds(pl.multiple_of(i * jtile, jtile), jtile)
             xs2[way, at, :] = (xk[part, at, :] + xr1[way, 1, at, :].astype(F32)).astype(BF)
 
-    copies(gra_r.at[:, :, :, left], rsem.at[10]).wait()
-    copies(gra_r.at[:, :, :, right], rsem.at[11]).wait()
+    arrived(30, gra_r)
     part = local_sum(wflip)
     xs1[0, 1] = part[:, :half].astype(BF)
     xs1[1, 1] = part[:, half:].astype(BF)
@@ -501,7 +580,7 @@
             V((n_zc, 2, n_y, half), BF), V((n_zc, 2, n_y, half), BF), V((n_y, 2 * n_zc, half), BF),
             V((n_y, 2 * n_zc, half), BF), V((n_zc, 2, n_y, half), BF), V((n_y, 2 * n_zc, half), BF),
             V((n_y, 2 * n_zc, half), BF), V((n_zc, 2, n_y, half), BF), V((halos, width), BF), V((nodes, halos), BF),
-            V((nodes, width), F32), V((nodes, width), F32), V((8, ends), F32),
+            V((nodes, width), F32), V((nodes, width), F32), V((8, ends), F32), V((8, ends), F32),
             V((ends, slots), BF), V((slots, ends), BF), V((slots, nodes), BF), V((nodes, slots), BF),
             V((n_dom, SLOTS, width), BF), V((n_zc, n_y, SLOTS, half), BF), V((n_y, n_zc, SLOTS, half), BF),
             V((n_y, n_zc, SLOTS, width), BF),
@@ -514,7 +593,7 @@
             V((n_z, zrows + 8, width), BF), V((n_z, zrows + 8, width), BF),
             V((n_y, zrows + 8, width), BF), V((n_x, zrows + 8, width), F32), V((2, n_z, zrows, width), F32),
             pltpu.SemaphoreType.DMA((7,)), pltpu.SemaphoreType.DMA((7,)),
-            pltpu.SemaphoreType.DMA((24,)), pltpu.SemaphoreType.DMA((24,)),
+            pltpu.SemaphoreType.DMA((36,)), pltpu.SemaphoreType.DMA((36,)),
         ],
         compiler_params=pltpu.CompilerParams(
             collective_id=0, has_side_effects=True, vmem_limit_bytes=60 * 1024 * 1024

time: 85.5 us -> 81.9 us (0.958)
  Pallas kernels: 84.2 us -> 80.7 us
    pallas_call x1, Pallas kernels: 83.2 us -> 79.7 us  [per_device(): pl.pallas_call(functools.partial(kernel, n_y, n_zc, n_x), out_shape=(V((n...]
where the time goes in v5:
time: 81.9 us; the launch traced here: 81.3 us
  Pallas kernels  80.7 us (99%)
    pallas_call x1, Pallas kernels, per_device(): pl.pallas_call(functools.partial(kernel, n_y, n_zc, n_x), out_shape=(V((n...  79.7 us

profile of v5, /device:TPU:1, one launch (start us, length us, event | category | flops | bytes accessed | tf_op | source)
XLA Modules:
  0.0 81.3 jit_solution(16779759987789844519)
XLA Ops:
  0.6 79.7 %encode_decode.1 = (bf16[1024,256]{1,0:T(8,128)(2,1)S(1)}, f32[256,256]{1,0:T(8,128)S(1)}, f32[256,256]{1,0:T(8,128)S(1)}, f32[8,256]{1,0:T(8,128)S(1)}) custom-call(s32[2,256]{1,0:T(2,128)} %bitcast.8, s32[2,256]{1,0:T(2,128)} %bitcast.9, s32[2,128]{1,0:T(2,128)} %bitcast.10, s32[1,256]{1,0:T(1,128)} %bitcast.11, f32[1,256]{1,0:T(1,128)} %bitcast.12, ...), custom_call_target="tpu_custom_call" | custom-call | tf_op jit(solution)/shard_map/encode_decode/pallas_call | solution.py:564
  80.3 1.0 %put_out.1 = (bf16[1024,256]{1,0:T(8,128)(2,1)}, f32[256,256]{1,0:T(8,128)}, f32[256,256]{1,0:T(8,128)}, f32[1,256]{1,0:T(1,128)}, f32[1,256]{1,0:T(1,128)}) custom-call(bf16[1024,256]{1,0:T(8,128)(2,1)S(1)} %get-tuple-element.14.emb, f32[256,256]{1,0:T(8,128)S(1)} %get-tuple-element.15.ge, f32[256,256]{1,0:T(8,128)S(1)} %get-tuple-element.16.gd, ...), custom_call_target="tpu_custom_call" | custom-call | tf_op jit(solution)/shard_map/put_out/pallas_call | solution.py:607

commit v6 on v5

--- a/solution.py
+++ b/solution.py
@@ -78,7 +78,7 @@
     eo, er, hr, lab, b_enc, b_dec1, w_dec2,
     feats, hist, adji, adjh, wself, wnbr, wdec1,
     ids_s, ids_r1, ids_t, ids_r2,
-    hal_s, hal_r1, hal_t, hal_r2, hal_m, hal_u, hal_v, hal_w, halo, adjp,
+    hal_s, hal_r1, hal_t, hal_r2, hal_m, hal_u, hal_v, hal_w, halo, turn, back, adjp,
     inner, selfp, place, far_place,
     hot_e, hot_et, hot_g, hot_gt,
     fet_s, fet_a, fet_b, fet_r,
@@ -219,6 +219,10 @@
     std = ((((jo >> (lzc + 1)) << lzc) + (jo & (n_zc - 1))) << 1) + ((jo >> lzc) & 1)
     adjp[...] = nn(adjh[...], hot(ko == std)).astype(BF)
 
+    io, oo = iota((halos, halos), 1), iota((halos, halos), 0)
+    turn[...] = hot(io == ((oo & (n_zc - 1)) << (ly + 1)) + (((oo >> lzc) & 1) << ly) + (oo >> (lzc + 1)))
+    back[...] = hot(io == ((oo & (n_y - 1)) << (lzc + 1)) + (((oo >> ly) & 1) << lzc) + (oo >> (ly + 1)))
+
     for i in (4, 5, 6):
         loads[i].wait()
 
@@ -231,10 +235,7 @@
         hal_s[:, c] = picked[c * n_dom : (c + 1) * n_dom, :half].reshape(n_zc, n_y, half)
         hal_m[:, c] = picked[c * n_dom : (c + 1) * n_dom, half:].reshape(n_zc, n_y, half)
     along_zc(2, lambda p: hal_s.at[p], lambda m: hal_r1.at[m], hal_s.at[pl.ds(0, n_zc - 1)])
-    io, oo = iota((halos, halos), 1), iota((halos, halos), 0)
-    turn = hot(io == ((oo & (n_zc - 1)) << (ly + 1)) + (((oo >> lzc) & 1) << ly) + (oo >> (lzc + 1)))
-    back = hot(io == ((oo & (n_y - 1)) << (lzc + 1)) + (((oo >> ly) & 1) << lzc) + (oo >> (ly + 1)))
-    hal_u[...] = nn(turn, hal_m[...].reshape(halos, half)).astype(BF).reshape(n_y, 2 * n_zc, half)
+    hal_u[...] = nn(turn[...], hal_m[...].reshape(halos, half)).astype(BF).reshape(n_y, 2 * n_zc, half)
     along_y(22, lambda p: hal_u.at[p], lambda m: hal_v.at[m], hal_u.at[pl.ds(0, n_y - 1)])
 
     gtile = min(256, slots)
@@ -250,33 +251,34 @@
     by_y = (offset_at(prow >> lzc, n_y) + y) & (n_y - 1)
     by_zc = (offset_at(prow & (n_zc - 1), n_zc) + zc) & (n_zc - 1)
     asked_far = nn(hot(pcol == (by_y << lzc) + by_zc), ids_r2[...].reshape(n_dom, LANES))
-    for i in range(slots // gtile):
-        id_col = ids_column(asked_far[i * per : (i + 1) * per])
-        hot_g[i * gtile : (i + 1) * gtile, :] = hot(id_col == iota((gtile, nodes), 1).astype(F32))
+
+    def rows_named(tiles):
+        for i in tiles:
+            id_col = ids_column(asked_far[i * per : (i + 1) * per])
+            hot_g[i * gtile : (i + 1) * gtile, :] = hot(id_col == iota((gtile, nodes), 1).astype(F32))
+
+    tiles = slots // gtile
+    rows_named(range(tiles // 2))
 
     copies(hal_r1, rsem.at[2]).wait()
-    hal_t[...] = nn(turn, hal_r1[...].reshape(halos, half)).astype(BF).reshape(n_y, 2 * n_zc, half)
+    hal_t[...] = nn(turn[...], hal_r1[...].reshape(halos, half)).astype(BF).reshape(n_y, 2 * n_zc, half)
     along_y(3, lambda p: hal_t.at[p], lambda m: hal_r2.at[m], hal_t.at[pl.ds(0, n_y - 1)])
     copies(hal_v, rsem.at[22]).wait()
-    hal_m[...] = nn(back, hal_v[...].reshape(halos, half)).astype(BF).reshape(n_zc, 2, n_y, half)
+    hal_m[...] = nn(back[...], hal_v[...].reshape(halos, half)).astype(BF).reshape(n_zc, 2, n_y, half)
     along_zc(23, lambda p: hal_m.at[p], lambda m: hal_w.at[m], hal_m.at[pl.ds(0, n_zc - 1)])
+
+    rows_named(range(tiles // 2, tiles))
 
     copies(hal_r2, rsem.at[3]).wait()
     copies(hal_w, rsem.at[23]).wait()
     halo[:, :half] = hal_r2[...].reshape(halos, half)
-    halo[:, half:] = nn(turn, hal_w[...].reshape(halos, half)).astype(BF)
+    halo[:, half:] = nn(turn[...], hal_w[...].reshape(halos, half)).astype(BF)
 
     @pl.loop(0, nodes // tile)
     def _(i):
         at = pl.ds(pl.multiple_of(i * tile, tile), tile)
         agg = (inner[at, :] + nn(adjp[at, :], halo[...])).astype(BF)
         emb_o[at, :] = jnp.maximum(selfp[at, :] + nn(agg, wnbr[...]), 0.0).astype(BF)
-
-    @pl.loop(0, slots // gtile)
-    def _(i):
-        at = pl.ds(pl.multiple_of(i * gtile, gtile), gtile)
-        block = nn(hot_g[at, :], emb_o[...]).astype(BF)
-        fet_s[pl.ds(i * per, per)] = block.reshape(per, SLOTS, width)
 
     left, right = pl.ds(0, half), pl.ds(half, half)
 
@@ -304,9 +306,9 @@
             else:
                 pltpu.make_async_copy(source, goal, rsem.at[base + 2 * group]).start()
 
-    def first_hop_y(base, send, mid, group):
+    def first_hop_y(base, send, mid, group, places):
         zcs = pl.ds(group * zc_part, zc_part)
-        for p in range(n_y):
+        for p in places:
             source, goal = send.at[p, zcs, :, right], mid.at[y, zcs]
             if y_off[p]:
                 send_to(base + 1, y_at(p) * n_zc + zc, source, goal, base + 1 + 2 * group)
@@ -331,10 +333,11 @@
             else:
                 pltpu.make_async_copy(source, goal, rsem.at[base + 5]).start()
 
-    def second_hops(base, mid_a, mid_b, recv):
-        for group in range(2):
-            second_hop_y(base, mid_a, recv, group)
-            second_hop_zc(base, mid_b, recv, group)
+    def second_hops(base, mid_a, mid_b, recv, group):
+        second_hop_y(base, mid_a, recv, group)
+        second_hop_zc(base, mid_b, recv, group)
+        if group == 0:
+            return
         sent.append((base, mid_a.at[pl.ds(0, n_zc - 1)]))
         sent.append((base + 1, mid_b.at[pl.ds(0, n_y - 1)]))
         sent.append((base + 2, mid_b.at[pl.ds(0, n_y - 1)]))
@@ -345,9 +348,21 @@
         copies(recv.at[:, :, :, right], rsem.at[base + 5]).wait()
 
     fet_s4, gra_s4 = (send.reshape(n_y, n_zc, SLOTS, width) for send in (fet_s, gra_s))
-    for group in range(2):
-        first_hop_zc(24, fet_s4, fet_a, group)
-        first_hop_y(24, fet_s4, fet_b, group)
+    far_y, near_y = range(y_part), range(y_part, n_y)
+
+    def selected(select, rows, goal, low, high):
+        @pl.loop(low, high)
+        def _(i):
+            at = pl.ds(pl.multiple_of(i * gtile, gtile), gtile)
+            goal[pl.ds(i * per, per)] = nn(select[at, :], rows[...]).astype(BF).reshape(per, SLOTS, width)
+
+    selected(hot_g, emb_o, fet_s, 0, tiles // 2)
+    first_hop_zc(24, fet_s4, fet_a, 0)
+    first_hop_y(24, fet_s4, fet_b, 0, far_y)
+    selected(hot_g, emb_o, fet_s, tiles // 2, tiles)
+    first_hop_y(24, fet_s4, fet_b, 0, near_y)
+    first_hop_zc(24, fet_s4, fet_a, 1)
+    first_hop_y(24, fet_s4, fet_b, 1, range(n_y))
     place_col = column_of(place[0:1, :])
     etile = min(256, ends)
     for i in range(ends // etile):
@@ -362,7 +377,8 @@
 
     target = column_of(lab[...].astype(F32))
 
-    second_hops(24, fet_a, fet_b, fet_r)
+    second_hops(24, fet_a, fet_b, fet_r, 0)
+    second_hops(24, fet_a, fet_b, fet_r, 1)
 
     asked = ids_r2[...].reshape(n_dom, LANES).astype(F32)
     id_row = jnp.concatenate(
@@ -418,23 +434,20 @@
     gpair[:queries, :] = (dz * tail).astype(BF)
     gpair[queries:, :] = (dz * head).astype(BF)
 
-    @pl.loop(0, slots // gtile)
-    def _(i):
-        at = pl.ds(pl.multiple_of(i * gtile, gtile), gtile)
-        block = nn(hot_et[at, :], gpair[...]).astype(BF)
-        gra_s[pl.ds(i * per, per)] = block.reshape(per, SLOTS, width)
-
-    for group in range(2):
-        first_hop_y(30, gra_s4, gra_b, group)
+    selected(hot_et, gpair, gra_s, 0, tiles // 2)
+    first_hop_y(30, gra_s4, gra_b, 0, far_y)
 
     pair.wait_recv()
     for j in range(n_z):
         dz_s[j, :zrows] = (dc_s[core, j * zrows : (j + 1) * zrows] + dc_r[j * zrows : (j + 1) * zrows]).astype(BF)
         dz_s[j, zrows:] = (dc_s[core, crows:] + dc_r[crows:]).astype(BF)
     along_z(13, lambda p: dz_s.at[p], lambda m: dz_r.at[m], dz_s.at[pl.ds(0, n_z - 1)])
-
-    for group in range(2):
-        first_hop_zc(30, gra_s4, gra_a, group)
+    first_hop_zc(30, gra_s4, gra_a, 0)
+    selected(hot_et, gpair, gra_s, tiles // 2, tiles)
+    first_hop_y(30, gra_s4, gra_b, 0, near_y)
+
+    first_hop_zc(30, gra_s4, gra_a, 1)
+    first_hop_y(30, gra_s4, gra_b, 1, range(n_y))
 
     copies(dz_r, rsem.at[13]).wait()
     total = dz_r[0].astype(F32)
@@ -443,7 +456,8 @@
     zbuf[...] = total.astype(BF)
     along_y(14, lambda p: zbuf, lambda m: dy_r.at[m], dy_r.at[pl.ds(0, n_y - 1)])
 
-    second_hops(30, gra_a, gra_b, gra_r)
+    second_hops(30, gra_a, gra_b, gra_r, 0)
+    second_hops(30, gra_a, gra_b, gra_r, 1)
 
     copies(dy_r, rsem.at[14]).wait()
     total = dy_r[0].astype(F32)
@@ -458,6 +472,49 @@
     pltpu.make_async_copy(dbuf, dx_r.at[rep], rsem.at[15]).start()
     sent.append((15, dx_r.at[pl.ds(0, n_x - 1)]))
 
+    flip = rep + 1 - 2 * lax.rem(rep, 2)
+    wrap = 3 - rep
+    wflip = wrap + 1 - 2 * lax.rem(wrap, 2)
+    quarter = nodes // n_x
+    jtile = min(64, quarter)
+
+    crow = quarter // 2
+    chunks = [(ch, pl.ds(ch * crow, crow)) for ch in range(2)]
+
+    def local_sum(q, ch):
+        at = pl.ds(pl.multiple_of(q * quarter + ch * crow, crow), crow)
+        return nn(hot_gt[at, :], gra_r[...].reshape(slots, width))
+
+    def trade(index, source, goal, partner):
+        copy = pltpu.make_async_remote_copy(
+            src_ref=source, dst_ref=goal, send_sem=ssem.at[index], recv_sem=rsem.at[index],
+            device_id={"rep": partner}, device_id_type=MESH,
+        )
+        copy.start()
+        return copy
+
+    def joined(way, part, ch):
+        @pl.loop(0, crow // jtile)
+        def _(i):
+            at = pl.ds(pl.multiple_of(ch * crow + i * jtile, jtile), jtile)
+            xs2[way, at, :] = (xk[part, at, :] + xr1[way, 1, at, :].astype(F32)).astype(BF)
+
+    arrived(30, gra_r)
+    firsts, seconds = [], []
+    for ch, at in chunks:
+        part = local_sum(wflip, ch)
+        xs1[0, 1, at] = part[:, :half].astype(BF)
+        xs1[1, 1, at] = part[:, half:].astype(BF)
+        part = local_sum(flip, ch)
+        xs1[0, 0, at] = part[:, :half].astype(BF)
+        one = trade(36 + ch, xs1.at[0, :, at], xr1.at[0, :, at], flip)
+        xk[3, at] = part[:, half:]
+        part = local_sum(wrap, ch)
+        xs1[1, 0, at] = part[:, half:].astype(BF)
+        two = trade(38 + ch, xs1.at[1, :, at], xr1.at[1, :, at], wrap)
+        xk[2, at] = part[:, :half]
+        firsts.append((one, two))
+
     copies(dx_r, rsem.at[15]).wait()
     total = dx_r[0]
     for j in range(1, n_x):
@@ -466,51 +523,19 @@
     dc_r[:zrows] = total[:zrows]
     along_z(20, lambda p: dc_r.at[pl.ds(0, zrows)], lambda m: dg_r.at[core, m], dg_r.at[0, pl.ds(0, n_z - 1)])
 
-    flip = rep + 1 - 2 * lax.rem(rep, 2)
-    wrap = 3 - rep
-    wflip = wrap + 1 - 2 * lax.rem(wrap, 2)
-    quarter = nodes // n_x
-    jtile = min(64, quarter)
-
-    def local_sum(q):
-        at = pl.ds(pl.multiple_of(q * quarter, quarter), quarter)
-        return nn(hot_gt[at, :], gra_r[...].reshape(slots, width))
-
-    def trade(index, source, goal, partner):
-        copy = pltpu.make_async_remote_copy(
-            src_ref=source, dst_ref=goal, send_sem=ssem.at[index], recv_sem=rsem.at[index],
-            device_id={"rep": partner}, device_id_type=MESH,
-        )
-        copy.start()
-        return copy
-
-    def joined(way, part):
-        @pl.loop(0, quarter // jtile)
-        def _(i):
-            at = pl.ds(pl.multiple_of(i * jtile, jtile), jtile)
-            xs2[way, at, :] = (xk[part, at, :] + xr1[way, 1, at, :].astype(F32)).astype(BF)
-
-    arrived(30, gra_r)
-    part = local_sum(wflip)
-    xs1[0, 1] = part[:, :half].astype(BF)
-    xs1[1, 1] = part[:, half:].astype(BF)
-    part = local_sum(flip)
-    xs1[0, 0] = part[:, :half].astype(BF)
-    one = trade(16, xs1.at[0], xr1.at[0], flip)
-    xk[3] = part[:, half:]
-    part = local_sum(wrap)
-    xs1[1, 0] = part[:, half:].astype(BF)
-    two = trade(17, xs1.at[1], xr1.at[1], wrap)
-    xk[2] = part[:, :half]
-    part = local_sum(rep)
-    xk[0] = part[:, :half]
-    xk[1] = part[:, half:]
-    one.wait_recv()
-    joined(0, 2)
-    three = trade(18, xs2.at[0], xr2.at[0], wrap)
-    two.wait_recv()
-    joined(1, 3)
-    four = trade(19, xs2.at[1], xr2.at[1], flip)
+    for ch, at in chunks:
+        part = local_sum(rep, ch)
+        xk[0, at] = part[:, :half]
+        xk[1, at] = part[:, half:]
+    for ch, at in chunks:
+        one, two = firsts[ch]
+        one.wait_recv()
+        joined(0, 2, ch)
+        three = trade(40 + ch, xs2.at[0, at], xr2.at[0, at], wrap)
+        two.wait_recv()
+        joined(1, 3, ch)
+        four = trade(42 + ch, xs2.at[1, at], xr2.at[1, at], flip)
+        seconds.append((three, four))
 
     copies(dg_r.at[0], rsem.at[20]).wait()
     last = pltpu.make_async_remote_copy(
@@ -519,15 +544,18 @@
     )
     last.start()
 
-    three.wait_recv()
-    ge_o[:, :half] = xk[0] + xr1[0, 0].astype(F32) + xr2[0].astype(F32)
-    four.wait_recv()
-    ge_o[:, half:] = xk[1] + xr1[1, 0].astype(F32) + xr2[1].astype(F32)
+    for ch, at in chunks:
+        three, four = seconds[ch]
+        three.wait_recv()
+        ge_o[at, :half] = xk[0, at] + xr1[0, 0, at].astype(F32) + xr2[0, at].astype(F32)
+        four.wait_recv()
+        ge_o[at, half:] = xk[1, at] + xr1[1, 0, at].astype(F32) + xr2[1, at].astype(F32)
 
     drain()
     pair.wait_send()
-    for copy in (one, two, three, four):
-        copy.wait_send()
+    for pair_of in firsts + seconds:
+        for copy in pair_of:
+            copy.wait_send()
     last.wait()
     gd_o[...] = dg_r[...].reshape(width, width)
 
@@ -579,7 +607,7 @@
             V((n_zc, n_y, LANES), BF), V((n_zc, n_y, LANES), BF), V((n_y, n_zc, LANES), BF), V((n_y, n_zc, LANES), BF),
             V((n_zc, 2, n_y, half), BF), V((n_zc, 2, n_y, half), BF), V((n_y, 2 * n_zc, half), BF),
             V((n_y, 2 * n_zc, half), BF), V((n_zc, 2, n_y, half), BF), V((n_y, 2 * n_zc, half), BF),
-            V((n_y, 2 * n_zc, half), BF), V((n_zc, 2, n_y, half), BF), V((halos, width), BF), V((nodes, halos), BF),
+            V((n_y, 2 * n_zc, half), BF), V((n_zc, 2, n_y, half), BF), V((halos, width), BF), V((halos, halos), BF), V((halos, halos), BF), V((nodes, halos), BF),
             V((nodes, width), F32), V((nodes, width), F32), V((8, ends), F32), V((8, ends), F32),
             V((ends, slots), BF), V((slots, ends), BF), V((slots, nodes), BF), V((nodes, slots), BF),
             V((n_dom, SLOTS, width), BF), V((n_zc, n_y, SLOTS, half), BF), V((n_y, n_zc, SLOTS, half), BF),
@@ -593,7 +621,7 @@
             V((n_z, zrows + 8, width), BF), V((n_z, zrows + 8, width), BF),
             V((n_y, zrows + 8, width), BF), V((n_x, zrows + 8, width), F32), V((2, n_z, zrows, width), F32),
             pltpu.SemaphoreType.DMA((7,)), pltpu.SemaphoreType.DMA((7,)),
-            pltpu.SemaphoreType.DMA((36,)), pltpu.SemaphoreType.DMA((36,)),
+            pltpu.SemaphoreType.DMA((44,)), pltpu.SemaphoreType.DMA((44,)),
         ],
         compiler_params=pltpu.CompilerParams(
             collective_id=0, has_side_effects=True, vmem_limit_bytes=60 * 1024 * 1024

time: 81.9 us -> 80.5 us (0.983)
  Pallas kernels: 80.7 us -> 79.6 us
    pallas_call x1, Pallas kernels: 79.7 us -> 78.6 us  [per_device(): pl.pallas_call(functools.partial(kernel, n_y, n_zc, n_x), out_shape=(V((n...]
where the time goes in v6:
time: 80.5 us; the launch traced here: 80.3 us
  Pallas kernels  79.6 us (99%)
    pallas_call x1, Pallas kernels, per_device(): pl.pallas_call(functools.partial(kernel, n_y, n_zc, n_x), out_shape=(V((n...  78.6 us

profile of v6, /device:TPU:1, one launch (start us, length us, event | category | flops | bytes accessed | tf_op | source)
XLA Modules:
  0.0 80.3 jit_solution(6741784847929226225)
XLA Ops:
  0.6 78.6 %encode_decode.1 = (bf16[1024,256]{1,0:T(8,128)(2,1)S(1)}, f32[256,256]{1,0:T(8,128)S(1)}, f32[256,256]{1,0:T(8,128)S(1)}, f32[8,256]{1,0:T(8,128)S(1)}) custom-call(s32[2,256]{1,0:T(2,128)} %bitcast.8, s32[2,256]{1,0:T(2,128)} %bitcast.9, s32[2,128]{1,0:T(2,128)} %bitcast.10, s32[1,256]{1,0:T(1,128)} %bitcast.11, f32[1,256]{1,0:T(1,128)} %bitcast.12, ...), custom_call_target="tpu_custom_call" | custom-call | tf_op jit(solution)/shard_map/encode_decode/pallas_call | solution.py:592
  79.3 1.0 %put_out.1 = (bf16[1024,256]{1,0:T(8,128)(2,1)}, f32[256,256]{1,0:T(8,128)}, f32[256,256]{1,0:T(8,128)}, f32[1,256]{1,0:T(1,128)}, f32[1,256]{1,0:T(1,128)}) custom-call(bf16[1024,256]{1,0:T(8,128)(2,1)S(1)} %get-tuple-element.14.emb, f32[256,256]{1,0:T(8,128)S(1)} %get-tuple-element.15.ge, f32[256,256]{1,0:T(8,128)S(1)} %get-tuple-element.16.gd, ...), custom_call_target="tpu_custom_call" | custom-call | tf_op jit(solution)/shard_map/put_out/pallas_call | solution.py:635

commit v7 on v6

--- a/solution.py
+++ b/solution.py
@@ -78,7 +78,7 @@
     eo, er, hr, lab, b_enc, b_dec1, w_dec2,
     feats, hist, adji, adjh, wself, wnbr, wdec1,
     ids_s, ids_r1, ids_t, ids_r2,
-    hal_s, hal_r1, hal_t, hal_r2, hal_m, hal_u, hal_v, hal_w, halo, turn, back, adjp,
+    hal_s, hal_r1, hal_t, hal_r2, hal_m, hal_u, hal_v, hal_w, turn, back, adjp, adjq,
     inner, selfp, place, far_place,
     hot_e, hot_et, hot_g, hot_gt,
     fet_s, fet_a, fet_b, fet_r,
@@ -218,6 +218,8 @@
     ko, jo = iota((halos, halos), 0), iota((halos, halos), 1)
     std = ((((jo >> (lzc + 1)) << lzc) + (jo & (n_zc - 1))) << 1) + ((jo >> lzc) & 1)
     adjp[...] = nn(adjh[...], hot(ko == std)).astype(BF)
+    std = ((((jo & (n_y - 1)) << lzc) + (jo >> (ly + 1))) << 1) + ((jo >> ly) & 1)
+    adjq[...] = nn(adjh[...], hot(ko == std)).astype(BF)
 
     io, oo = iota((halos, halos), 1), iota((halos, halos), 0)
     turn[...] = hot(io == ((oo & (n_zc - 1)) << (ly + 1)) + (((oo >> lzc) & 1) << ly) + (oo >> (lzc + 1)))
@@ -271,13 +273,12 @@
 
     copies(hal_r2, rsem.at[3]).wait()
     copies(hal_w, rsem.at[23]).wait()
-    halo[:, :half] = hal_r2[...].reshape(halos, half)
-    halo[:, half:] = nn(turn[...], hal_w[...].reshape(halos, half)).astype(BF)
 
     @pl.loop(0, nodes // tile)
     def _(i):
         at = pl.ds(pl.multiple_of(i * tile, tile), tile)
-        agg = (inner[at, :] + nn(adjp[at, :], halo[...])).astype(BF)
+        outer = [nn(adjp[at, :], hal_r2[...].reshape(halos, half)), nn(adjq[at, :], hal_w[...].reshape(halos, half))]
+        agg = (inner[at, :] + jnp.concatenate(outer, axis=1)).astype(BF)
         emb_o[at, :] = jnp.maximum(selfp[at, :] + nn(agg, wnbr[...]), 0.0).astype(BF)
 
     left, right = pl.ds(0, half), pl.ds(half, half)
@@ -607,7 +608,7 @@
             V((n_zc, n_y, LANES), BF), V((n_zc, n_y, LANES), BF), V((n_y, n_zc, LANES), BF), V((n_y, n_zc, LANES), BF),
             V((n_zc, 2, n_y, half), BF), V((n_zc, 2, n_y, half), BF), V((n_y, 2 * n_zc, half), BF),
             V((n_y, 2 * n_zc, half), BF), V((n_zc, 2, n_y, half), BF), V((n_y, 2 * n_zc, half), BF),
-            V((n_y, 2 * n_zc, half), BF), V((n_zc, 2, n_y, half), BF), V((halos, width), BF), V((halos, halos), BF), V((halos, halos), BF), V((nodes, halos), BF),
+            V((n_y, 2 * n_zc, half), BF), V((n_zc, 2, n_y, half), BF), V((halos, halos), BF), V((halos, halos), BF), V((nodes, halos), BF), V((nodes, halos), BF),
             V((nodes, width), F32), V((nodes, width), F32), V((8, ends), F32), V((8, ends), F32),
             V((ends, slots), BF), V((slots, ends), BF), V((slots, nodes), BF), V((nodes, slots), BF),
             V((n_dom, SLOTS, width), BF), V((n_zc, n_y, SLOTS, half), BF), V((n_y, n_zc, SLOTS, half), BF),

time: 80.5 us -> 80.4 us (level)
  no operation moved by 1% of the time
where the time goes in v7:
time: 80.4 us; the launch traced here: 80.2 us
  Pallas kernels  79.5 us (99%)
    pallas_call x1, Pallas kernels, per_device(): pl.pallas_call(functools.partial(kernel, n_y, n_zc, n_x), out_shape=(V((n...  78.5 us

profile of v7, /device:TPU:1, one launch (start us, length us, event | category | flops | bytes accessed | tf_op | source)
XLA Modules:
  0.0 80.2 jit_solution(14763538105279690683)
XLA Ops:
  0.6 78.5 %encode_decode.1 = (bf16[1024,256]{1,0:T(8,128)(2,1)S(1)}, f32[256,256]{1,0:T(8,128)S(1)}, f32[256,256]{1,0:T(8,128)S(1)}, f32[8,256]{1,0:T(8,128)S(1)}) custom-call(s32[2,256]{1,0:T(2,128)} %bitcast.8, s32[2,256]{1,0:T(2,128)} %bitcast.9, s32[2,128]{1,0:T(2,128)} %bitcast.10, s32[1,256]{1,0:T(1,128)} %bitcast.11, f32[1,256]{1,0:T(1,128)} %bitcast.12, ...), custom_call_target="tpu_custom_call" | custom-call | tf_op jit(solution)/shard_map/encode_decode/pallas_call | solution.py:593
  79.2 1.0 %put_out.1 = (bf16[1024,256]{1,0:T(8,128)(2,1)}, f32[256,256]{1,0:T(8,128)}, f32[256,256]{1,0:T(8,128)}, f32[1,256]{1,0:T(1,128)}, f32[1,256]{1,0:T(1,128)}) custom-call(bf16[1024,256]{1,0:T(8,128)(2,1)S(1)} %get-tuple-element.14.emb, f32[256,256]{1,0:T(8,128)S(1)} %get-tuple-element.15.ge, f32[256,256]{1,0:T(8,128)S(1)} %get-tuple-element.16.gd, ...), custom_call_target="tpu_custom_call" | custom-call | tf_op jit(solution)/shard_map/put_out/pallas_call | solution.py:636
